TPU v7x, 512 devices: a whole 4x8x8 slice. The times are simulated.
512 devices in a mesh: wide: 64 (over y, x, z_hi), narrow: 8 (over z_lo, core).
Axes of the slice: x: 4, y: 8, z: 8 (z_hi: 2, z_lo: 4; z = z_hi * 4 + z_lo), core: 2. Of those that a mesh axis runs over, the one named last changes fastest.
Arguments:
- context: bfloat16 [65536, 3072], P('wide', 'narrow'), may hold values from -6 to 6
- out_weight: bfloat16 [3072, 6144], P('wide', 'narrow'), may hold values from -0.109375 to 0.109375
- residual: bfloat16 [65536, 6144], P('wide', 'narrow'), may hold values from -180 to 180
- ln_gain: bfloat16 [6144], P('narrow'), may hold values from 0.5 to 1.5
- side_down: bfloat16 [6144, 768], P('narrow', 'wide'), may hold values from -0.078125 to 0.078125
- f_weight: bfloat16 [384, 384], replicated, may hold values from -0.3125 to 0.3125
- g_weight: bfloat16 [384, 384], replicated, may hold values from -0.3125 to 0.3125
- targets: float32 [65536, 768], P(('wide', 'narrow')), may hold values from -18 to 18
Outputs:
- side_out: float32 [65536, 768], P(('wide', 'narrow'))
- f_grad: float32 [384, 384], replicated
- g_grad: float32 [384, 384], replicated
All inputs are finite; a program needn't handle non-finite values.
Results may differ from a plain program's by a relative error of at most 0.00035.
The roundings to bfloat16 on the way count: a program that leaves them out, or rounds other values in their place, can miss the bound.
Values may be sent and summed in bfloat16 or wider, within the bound.
A program may use at most 64 MiB of HBM per device.

v0:
```python
import jax
import jax.numpy as jnp
from jax import lax
from jax.sharding import PartitionSpec as P


def coupling(values, weight):
    return jax.nn.gelu(jnp.dot(values, weight, precision=lax.Precision.HIGHEST))


def per_device(context, out_weight, residual, ln_gain, side_down, f_weight, g_weight, targets):
    full_weight = lax.all_gather(out_weight, "wide", axis=0, tiled=True)
    whole = lax.all_gather(context, "narrow", axis=1, tiled=True)
    attn_sum = jnp.dot(whole, full_weight, preferred_element_type=jnp.float32)
    stream = (residual.astype(jnp.float32) + attn_sum).astype(jnp.bfloat16)
    stream_value = stream.astype(jnp.float32)
    row_sum = jnp.sum(stream_value, axis=1)
    row_squares = jnp.sum(stream_value * stream_value, axis=1)
    scaled = (stream_value * ln_gain.astype(jnp.float32)[None, :]).astype(jnp.bfloat16)
    down_full = lax.all_gather(side_down, "wide", axis=1, tiled=True)
    gain_part = jnp.dot(ln_gain[None, :], down_full, preferred_element_type=jnp.float32)[0]
    local_rows = targets.shape[0]
    sums_all, squares_all, gain_map = lax.psum((row_sum, row_squares, gain_part), "narrow")
    offset = lax.axis_index("narrow") * local_rows
    token_sum = lax.dynamic_slice_in_dim(sums_all, offset, local_rows, 0)
    token_squares = lax.dynamic_slice_in_dim(squares_all, offset, local_rows, 0)
    projected = lax.psum_scatter(
        jnp.dot(scaled, down_full, preferred_element_type=jnp.float32),
        "narrow",
        scatter_dimension=0,
        tiled=True,
    )
    features = stream.shape[1] * lax.axis_size("narrow")
    mean = token_sum / features
    spread = token_squares / features - mean * mean
    side_in = (projected - mean[:, None] * gain_map[None, :]) / jnp.sqrt(spread + 1e-06)[:, None]
    half = side_in.shape[1] // 2
    f_w = f_weight.astype(jnp.float32)
    g_w = g_weight.astype(jnp.float32)
    first = side_in[:, :half]
    second = side_in[:, half:]
    upper = first + coupling(second, f_w)
    g_value, g_pull = jax.vjp(coupling, upper, g_w)
    lower = second + g_value
    side_out = jnp.concatenate([upper, lower], axis=1)
    all_tokens = local_rows * lax.axis_size("wide") * lax.axis_size("narrow")
    misfit = (side_out - targets) / all_tokens
    upper_back, g_local = g_pull(misfit[:, half:])
    rebuilt = lower - g_value
    upper_total = misfit[:, :half] + upper_back
    f_value, f_pull = jax.vjp(coupling, rebuilt, f_w)
    f_local = f_pull(upper_total)[1]
    f_total, g_total = lax.psum((f_local, g_local), ("wide", "narrow"))
    return (side_out, f_total, g_total)


def solution(mesh):
    in_specs = (
        P("wide", "narrow"),
        P("wide", "narrow"),
        P("wide", "narrow"),
        P("narrow"),
        P("narrow", "wide"),
        P(),
        P(),
        P(("wide", "narrow"), None),
    )
    out_specs = (P(("wide", "narrow"), None), P(), P())
    return jax.shard_map(
        per_device, mesh=mesh, in_specs=in_specs, out_specs=out_specs, check_vma=False
    )
```

profile of v0, /device:TPU:1, one launch (start us, length us, event | category | flops | bytes accessed | tf_op | source)
XLA Modules:
  0.0 738.7 jit_solution(3532235506291187647)
XLA Ops:
  7.2 0.7 all-gather.9.cloned.1.call-update
  8.0 0.7 all-gather.7.cloned.1.call-update
  8.7 0.7 all-gather.5.cloned.1.call-update
  9.5 1.7 copy.13
  11.2 135.7 %all-gather.9.cloned.1.call-done = bf16[64,12,768]{2,1,0:T(8,128)(2,1)} async-done(((bf16[1,12,768]{2,1,0:T(8,128)(2,1)}), bf16[64,12,768]{2,1,0:T(8,128)(2,1)}) %all-gather.9.cloned.1.call-update) | async-done | bytes 1179664 | tf_op jit(solution)/shard_map/all_gather | solution.py:20
  146.9 2.2 reshape.15
  149.2 158.8 %all-gather.7.cloned.1.call-done = bf16[3072,768]{1,0:T(8,128)(2,1)} async-done(((bf16[48,768]{1,0:T(8,128)(2,1)}), bf16[3072,768]{1,0:T(8,128)(2,1)}) %all-gather.7.cloned.1.call-update) | async-done | bytes 4718608 | tf_op jit(solution)/shard_map/all_gather | solution.py:12
  308.0 74.8 %all-gather.5.cloned.1.call-done = bf16[1024,3072]{1,0:T(8,128)(2,1)} async-done(((bf16[1024,384]{1,0:T(8,128)(2,1)}), bf16[1024,3072]{1,0:T(8,128)(2,1)}) %all-gather.5.cloned.1.call-update) | async-done | bytes 6291472 | tf_op jit(solution)/shard_map/all_gather | solution.py:13
  382.8 8.9 %convert_reduce_fusion = (f32[1024]{0:T(1024)S(1)}, f32[1024]{0:T(1024)S(1)}, bf16[1024,768]{0,1:T(8,128)(2,1)S(1)}) fusion(bf16[1024,3072]{1,0:T(8,128)(2,1)} %all-gather.5.cloned.1.call-done, bf16[3072,768]{1,0:T(8,128)(2,1)} %all-gather.7.cloned.1.call-done, bf16[1024,768]{0,1:T(8,128)(2,1)S(1)} %copy.13), kind=kOutput, calls=%fused_computation.1 | convolution fusion | flops 4837341184 | bytes 14163968 | tf_op jit(solution)/shard_map/dot_general | solution.py:14
  391.6 3.3 fusion.2
  395.0 0.4 fusion.7
  395.5 25.3 %all-reduce.1 = (f32[1024]{0:T(1024)S(1)}, f32[1024]{0:T(1024)S(1)}, f32[768]{0:T(1024)S(1)}) all-reduce(f32[1024]{0:T(1024)S(1)} %get-tuple-element.4, f32[1024]{0:T(1024)S(1)} %get-tuple-element.3, f32[768]{0:T(1024)S(1)} %fusion.7), channel_id=1, replica_groups=mesh['wide'=64,'narrow'=8] {'narrow'}, use_global_device_ids=true, to_apply=%region_5.0 | all-reduce | flops 2816 | bytes 22528 | tf_op jit(solution)/shard_map/psum | solution.py:23
  420.8 22.0 %reduce-scatter.2.cloned.1.call-done = f32[128,768]{1,0:T(8,128)} async-done(((f32[1024,768]{1,0:T(8,128)}), f32[128,768]{1,0:T(8,128)}) %reduce-scatter.2.cloned.1.call-update) | async-done | bytes 393232 | tf_op jit(solution)/shard_map/reduce_scatter | solution.py:27
  442.8 1.1 subtract_divide_fusion
  443.9 0.4 fusion.31
  444.3 0.4 slice_add_fusion
  444.7 0.8 subtract_multiply_fusion
  445.5 1.6 fusion.64
  447.0 0.5 convolution_add_fusion
  447.5 0.4 fusion.62
  448.0 1.6 fusion.22
  449.6 278.8 %all-reduce.4.cloned.1.call-done = (f32[384,384]{1,0:T(8,128)}, f32[384,384]{1,0:T(8,128)}) async-done(((f32[384,384]{1,0:T(8,128)}, f32[384,384]{1,0:T(8,128)}), (f32[384,384]{1,0:T(8,128)}, f32[384,384]{1,0:T(8,128)})) %all-reduce.4.cloned.1.call-update) | async-done | bytes 1179664 | tf_op jit(solution)/shard_map/psum | solution.py:53
  728.4 1.9 copy.16
  730.3 1.9 copy.17
  (18 shorter events, 0.3 us)
Async XLA Ops:
  7.2 437.1 %copy-start = (bf16[384,384]{1,0:T(8,128)(2,1)S(1)}, bf16[384,384]{1,0:T(8,128)(2,1)}, u32[]{:S(2)}) copy-start(bf16[384,384]{1,0:T(8,128)(2,1)} %param.14) | copy-start | bytes 884740
  7.2 4.0 copy-start.3
  7.2 139.8 %all-gather.9.cloned.1.call-start = ((), (), s32[]{:S(2)}) async-start(), calls=%async_computation.4 | async-start | bytes 1597440 | tf_op jit(solution)/shard_map/all_gather | solution.py:20
  7.9 300.1 %all-gather.7.cloned.1.call-start = ((), (), s32[]{:S(2)}) async-start(), calls=%async_computation.2 | async-start | bytes 4792320 | tf_op jit(solution)/shard_map/all_gather | solution.py:12
  8.7 374.1 %all-gather.5.cloned.1.call-start = ((), (), s32[]{:S(2)}) async-start(), calls=%async_computation.1 | async-start | bytes 7077888 | tf_op jit(solution)/shard_map/all_gather | solution.py:13
  9.4 433.4 %reduce-scatter.2.cloned.1.call-start = ((), (), s32[]{:S(2)}) async-start(), calls=%async_computation.3 | async-start | bytes 3538944 | tf_op jit(solution)/shard_map/reduce_scatter | solution.py:27
  394.9 49.0 %copy-start.2 = (bf16[384,384]{1,0:T(8,128)(2,1)S(1)}, bf16[384,384]{1,0:T(8,128)(2,1)}, u32[]{:S(2)}) copy-start(bf16[384,384]{1,0:T(8,128)(2,1)} %param.13) | copy-start | bytes 884740
  394.9 49.8 %copy-start.1 = (f32[128,768]{1,0:T(8,128)S(1)}, f32[128,768]{1,0:T(8,128)}, u32[]{:S(2)}) copy-start(f32[128,768]{1,0:T(8,128)} %param.15) | copy-start | bytes 1179652
  394.9 333.4 %all-reduce.4.cloned.1.call-start = ((), (), s32[]{:S(2)}) async-start(), calls=%async_computation.5 | async-start | bytes 2359296 | tf_op jit(solution)/shard_map/psum | solution.py:53
Sparse Core Ops, SparseCore 0:
  12.4 134.4 all-gather.8
  151.4 156.5 all-gather.6
  310.1 72.6 all-gather.4
  395.0 47.6 reduce-scatter.1
  449.7 278.5 all-reduce.3
where the time goes:
time: 739 us
  waiting for transfers between devices  672 us (91%)
  blocking collectives  25.3 us (3%)
  matrix products  17.4 us (2%)
  between operations  13.9 us (2%)
  local copies, waits for them, and re-layouts  7.82 us (1%)
    psum x1, waiting for transfers between devices, per_device(): f_total, g_total = lax.psum((f_local, g_local), ('wide', 'narrow'))  279 us
    all_gather x1, waiting for transfers between devices, per_device(): full_weight = lax.all_gather(out_weight, 'wide', axis=0, tiled=True)  159 us
    all_gather x1, waiting for transfers between devices, per_device(): down_full = lax.all_gather(side_down, 'wide', axis=1, tiled=True)  136 us
    all_gather x1, waiting for transfers between devices, per_device(): whole = lax.all_gather(context, 'narrow', axis=1, tiled=True)  74.8 us
    psum x1, blocking collectives, per_device(): lax.psum((row_sum, row_squares, gain_part), 'narrow')  25.3 us
    reduce_scatter x1, waiting for transfers between devices, per_device(): lax.psum_scatter(jnp.dot(scaled, down_full, preferred_element_type=jnp.fl...  22 us
  transfers between devices with their start and end apart: 5, of which 5 were waited for; matrix products, arithmetic and copies ran while one was open for 1% of the time, Pallas kernels for 0%

commit v1 on v0

--- a/solution.py
+++ b/solution.py
@@ -1,7 +1,137 @@
 import jax
 import jax.numpy as jnp
 from jax import lax
+from jax.experimental import pallas as pl
+from jax.experimental.pallas import tpu as pltpu
 from jax.sharding import PartitionSpec as P
+
+MESH = pl.DeviceIdType.MESH
+
+
+def position():
+    w = lax.axis_index("wide")
+    n = lax.axis_index("narrow")
+    return w // 8, (w // 2) % 4, (w % 2) * 4 + n // 2, n % 2
+
+
+def device(y, x, z, c):
+    return ((y * 4 + x) * 2 + z // 4, (z % 4) * 2 + c)
+
+
+def ar_kernel(f_ref, g_ref, f_out, g_out, buf0, half, buf_a, mid, buf_b, buf_x, tail, fin, sems_s, sems_r):
+    y, x, z, c = position()
+    on_z = 1 - c
+    pos_a = z * on_z + y * c
+    pos_b = y * on_z + z * c
+
+    def along_a(d):
+        return device((y + d * c) % 8, x, (z + d * on_z) % 8, c)
+
+    def along_b(d):
+        return device((y + d * on_z) % 8, x, (z + d * c) % 8, c)
+
+    def along_x(d):
+        return device(y, (x + d) % 4, z, c)
+
+    sibling = device(y, x, z, 1 - c)
+    barrier = pltpu.get_barrier_semaphore()
+    partners = [sibling] + [along_a(d) for d in range(1, 8)] + [along_b(d) for d in range(1, 8)] + [along_x(d) for d in range(1, 4)]
+    for partner in partners:
+        pl.semaphore_signal(barrier, inc=1, device_id=partner, device_id_type=MESH)
+    pl.semaphore_wait(barrier, len(partners))
+    sent = []
+
+    def send(src, dst, slot, to):
+        copy = pltpu.make_async_remote_copy(
+            src_ref=src, dst_ref=dst, send_sem=sems_s.at[slot], recv_sem=sems_r.at[slot], device_id=to, device_id_type=MESH
+        )
+        copy.start()
+        sent.append(copy)
+        return copy
+
+    def own(total, mine):
+        copy = pltpu.make_async_remote_copy(
+            src_ref=mine, dst_ref=buf0, send_sem=sems_s.at[0], recv_sem=sems_r.at[0], device_id=sibling, device_id_type=MESH
+        )
+        copy.start()
+        copy.wait()
+        half[...] = total[...] + buf0[...]
+
+    @pl.when(c == 0)
+    def _():
+        own(f_ref, g_ref)
+
+    @pl.when(c == 1)
+    def _():
+        own(g_ref, f_ref)
+
+    def rows(ref, at, n):
+        return ref.at[pl.ds(pl.multiple_of(at * n, 8), n)]
+
+    copies = [
+        send(rows(half, (pos_a + d) % 8, 48), buf_a.at[d - 1], d, along_a(d)) for d in range(1, 8)
+    ]
+    total = half[pl.ds(pl.multiple_of(pos_a * 48, 8), 48), :]
+    for d in range(1, 8):
+        copies[d - 1].wait_recv()
+        total = total + buf_a[d - 1]
+    mid[0:48, :] = total
+    mid[48:64, :] = jnp.zeros((16, 384), jnp.float32)
+    copies = [
+        send(rows(mid, (pos_b + d) % 8, 8), buf_b.at[d - 1], 7 + d, along_b(d)) for d in range(1, 8)
+    ]
+    total = mid[pl.ds(pl.multiple_of(pos_b * 8, 8), 8), :]
+    for d in range(1, 8):
+        copies[d - 1].wait_recv()
+        total = total + buf_b[d - 1]
+    buf_x[x] = total
+    copies = [send(buf_x.at[x], buf_x.at[x], 14 + d, along_x(d)) for d in range(1, 4)]
+    for copy in copies:
+        copy.wait_recv()
+    tail[pl.ds(pl.multiple_of(pos_b * 8, 8), 8), :] = (buf_x[0] + buf_x[1]) + (buf_x[2] + buf_x[3])
+    copies = [send(rows(tail, pos_b, 8), rows(tail, pos_b, 8), 17 + d, along_b(d)) for d in range(1, 8)]
+    for copy in copies:
+        copy.wait_recv()
+    place = pl.ds(pl.multiple_of(pos_a * 48, 8), 48)
+    copies = [send(tail.at[pl.ds(0, 48)], fin.at[c, place], 24 + d, along_a(d)) for d in range(1, 8)]
+    shares = [send(tail.at[pl.ds(0, 48)], fin.at[c, place], 32, sibling)]
+    fin[c, place, :] = tail[0:48, :]
+    for d in range(1, 8):
+        copies[d - 1].wait_recv()
+        there = pl.ds(pl.multiple_of((pos_a + 8 - d) % 8 * 48, 8), 48)
+        shares.append(send(fin.at[c, there], fin.at[c, there], 32 + d, sibling))
+    for copy in shares:
+        copy.wait_recv()
+    f_out[...] = fin[0]
+    g_out[...] = fin[1]
+    for copy in sent:
+        copy.wait_send()
+
+
+def all_reduce(f_local, g_local):
+    size = f_local.shape[0]
+    vmem = pl.BlockSpec(memory_space=pltpu.VMEM)
+    full = jax.ShapeDtypeStruct((size, size), jnp.float32)
+    return pl.pallas_call(
+        ar_kernel,
+        out_shape=(full, full),
+        in_specs=[vmem, vmem],
+        out_specs=(vmem, vmem),
+        scratch_shapes=[
+            pltpu.VMEM((size, size), jnp.float32),
+            pltpu.VMEM((size, size), jnp.float32),
+            pltpu.VMEM((7, size // 8, size), jnp.float32),
+            pltpu.VMEM((64, size), jnp.float32),
+            pltpu.VMEM((7, 8, size), jnp.float32),
+            pltpu.VMEM((4, 8, size), jnp.float32),
+            pltpu.VMEM((64, size), jnp.float32),
+            pltpu.VMEM((2, size, size), jnp.float32),
+            pltpu.SemaphoreType.DMA((40,)),
+            pltpu.SemaphoreType.DMA((40,)),
+        ],
+        compiler_params=pltpu.CompilerParams(collective_id=1, has_side_effects=True),
+        name="gradient_sum",
+    )(f_local, g_local)
 
 
 def coupling(values, weight):
@@ -50,7 +180,7 @@
     upper_total = misfit[:, :half] + upper_back
     f_value, f_pull = jax.vjp(coupling, rebuilt, f_w)
     f_local = f_pull(upper_total)[1]
-    f_total, g_total = lax.psum((f_local, g_local), ("wide", "narrow"))
+    f_total, g_total = all_reduce(f_local, g_local)
     return (side_out, f_total, g_total)
 
 

time: 739 us -> 511 us (0.69)
  waiting for transfers between devices: 672 us -> 393 us
  Pallas kernels: 0 us -> 49.6 us
    psum x1 -> x0, waiting for transfers between devices: 279 us -> none  [per_device(): f_total, g_total = lax.psum((f_local, g_local), ('wide', 'narrow'))]
    pallas_call x0 -> x1, Pallas kernels: none -> 49.6 us  [all_reduce(): pl.pallas_call(ar_kernel, out_shape=(full, full), in_specs=[vmem, vmem],...]
  transfers between devices with their start and end apart: 5 -> 4, of which waited for: 5 -> 4; matrix products, arithmetic and copies ran while one was open for 1% -> 1% of each run, Pallas kernels for 0% -> 0%
where the time goes in v1:
time: 511 us; the launch traced here: 510 us
  waiting for transfers between devices  393 us (77%)
  Pallas kernels  49.6 us (10%)
  blocking collectives  25.3 us (5%)
  matrix products  17.4 us (3%)
  between operations  13.9 us (3%)
  local copies, waits for them, and re-layouts  7.82 us (2%)
    all_gather x1, waiting for transfers between devices, per_device(): full_weight = lax.all_gather(out_weight, 'wide', axis=0, tiled=True)  159 us
    all_gather x1, waiting for transfers between devices, per_device(): down_full = lax.all_gather(side_down, 'wide', axis=1, tiled=True)  136 us
    all_gather x1, waiting for transfers between devices, per_device(): whole = lax.all_gather(context, 'narrow', axis=1, tiled=True)  74.8 us
    pallas_call x1, Pallas kernels, all_reduce(): pl.pallas_call(ar_kernel, out_shape=(full, full), in_specs=[vmem, vmem],...  49.6 us
    psum x1, blocking collectives, per_device(): lax.psum((row_sum, row_squares, gain_part), 'narrow')  25.3 us
    reduce_scatter x1, waiting for transfers between devices, per_device(): lax.psum_scatter(jnp.dot(scaled, down_full, preferred_element_type=jnp.fl...  22 us
  transfers between devices with their start and end apart: 4, of which 4 were waited for; matrix products, arithmetic and copies ran while one was open for 1% of the time, Pallas kernels for 0%

profile of v1, /device:TPU:1, one launch (start us, length us, event | category | flops | bytes accessed | tf_op | source)
XLA Modules:
  0.0 509.5 jit_solution(3209444905790959562)
XLA Ops:
  7.2 0.7 all-gather.9.cloned.1.call-update
  8.0 0.7 all-gather.7.cloned.1.call-update
  8.7 0.7 all-gather.5.cloned.1.call-update
  9.5 1.7 copy.13
  11.2 135.7 %all-gather.9.cloned.1.call-done = bf16[64,12,768]{2,1,0:T(8,128)(2,1)} async-done(((bf16[1,12,768]{2,1,0:T(8,128)(2,1)}), bf16[64,12,768]{2,1,0:T(8,128)(2,1)}) %all-gather.9.cloned.1.call-update) | async-done | bytes 1179664 | tf_op jit(solution)/shard_map/all_gather | solution.py:150
  146.9 2.2 reshape.15
  149.2 158.8 %all-gather.7.cloned.1.call-done = bf16[3072,768]{1,0:T(8,128)(2,1)} async-done(((bf16[48,768]{1,0:T(8,128)(2,1)}), bf16[3072,768]{1,0:T(8,128)(2,1)}) %all-gather.7.cloned.1.call-update) | async-done | bytes 4718608 | tf_op jit(solution)/shard_map/all_gather | solution.py:142
  308.0 74.8 %all-gather.5.cloned.1.call-done = bf16[1024,3072]{1,0:T(8,128)(2,1)} async-done(((bf16[1024,384]{1,0:T(8,128)(2,1)}), bf16[1024,3072]{1,0:T(8,128)(2,1)}) %all-gather.5.cloned.1.call-update) | async-done | bytes 6291472 | tf_op jit(solution)/shard_map/all_gather | solution.py:143
  382.8 8.9 %convert_reduce_fusion = (f32[1024]{0:T(1024)S(1)}, f32[1024]{0:T(1024)S(1)}, bf16[1024,768]{0,1:T(8,128)(2,1)S(1)}) fusion(bf16[1024,3072]{1,0:T(8,128)(2,1)} %all-gather.5.cloned.1.call-done, bf16[3072,768]{1,0:T(8,128)(2,1)} %all-gather.7.cloned.1.call-done, bf16[1024,768]{0,1:T(8,128)(2,1)S(1)} %copy.13), kind=kOutput, calls=%fused_computation.1 | convolution fusion | flops 4837341184 | bytes 14163968 | tf_op jit(solution)/shard_map/dot_general | solution.py:144
  391.6 3.3 fusion.2
  394.9 0.4 fusion.7
  395.4 25.3 %all-reduce = (f32[1024]{0:T(1024)S(1)}, f32[1024]{0:T(1024)S(1)}, f32[768]{0:T(1024)S(1)}) all-reduce(f32[1024]{0:T(1024)S(1)} %get-tuple-element.8, f32[1024]{0:T(1024)S(1)} %get-tuple-element.7, f32[768]{0:T(1024)S(1)} %fusion.7), channel_id=1, replica_groups=mesh['wide'=64,'narrow'=8] {'narrow'}, use_global_device_ids=true, to_apply=%region_5.0 | all-reduce | flops 2816 | bytes 22528 | tf_op jit(solution)/shard_map/psum | solution.py:153
  420.8 22.0 %reduce-scatter.2.cloned.1.call-done = f32[128,768]{1,0:T(8,128)} async-done(((f32[1024,768]{1,0:T(8,128)}), f32[128,768]{1,0:T(8,128)}) %reduce-scatter.2.cloned.1.call-update) | async-done | bytes 393232 | tf_op jit(solution)/shard_map/reduce_scatter | solution.py:157
  442.8 1.1 subtract_divide_fusion
  443.9 0.4 fusion.31
  444.3 0.4 slice_add_fusion
  444.7 0.8 subtract_multiply_fusion
  445.5 1.6 fusion.64.g_ref
  447.1 0.5 convolution_add_fusion
  447.5 0.4 fusion.62
  448.0 1.6 fusion.22.f_ref
  449.6 49.6 %gradient_sum.1 = (f32[384,384]{1,0:T(8,128)}, f32[384,384]{1,0:T(8,128)}) custom-call(f32[384,384]{1,0:T(8,128)} %fusion.22.f_ref, f32[384,384]{1,0:T(8,128)} %fusion.64.g_ref), custom_call_target="tpu_custom_call" | custom-call | tf_op jit(solution)/shard_map/gradient_sum/pallas_call | solution.py:115
  499.2 1.9 copy.16
  501.1 1.9 copy.17
  (16 shorter events, 0.3 us)
Async XLA Ops:
  7.2 437.1 %copy-start = (bf16[384,384]{1,0:T(8,128)(2,1)S(1)}, bf16[384,384]{1,0:T(8,128)(2,1)}, u32[]{:S(2)}) copy-start(bf16[384,384]{1,0:T(8,128)(2,1)} %param.14) | copy-start | bytes 884740
  7.2 4.0 copy-start.3
  7.2 139.8 %all-gather.9.cloned.1.call-start = ((), (), s32[]{:S(2)}) async-start(), calls=%async_computation.4 | async-start | bytes 1597440 | tf_op jit(solution)/shard_map/all_gather | solution.py:150
  7.9 300.1 %all-gather.7.cloned.1.call-start = ((), (), s32[]{:S(2)}) async-start(), calls=%async_computation.2 | async-start | bytes 4792320 | tf_op jit(solution)/shard_map/all_gather | solution.py:142
  8.7 374.1 %all-gather.5.cloned.1.call-start = ((), (), s32[]{:S(2)}) async-start(), calls=%async_computation.1 | async-start | bytes 7077888 | tf_op jit(solution)/shard_map/all_gather | solution.py:143
  9.4 433.4 %reduce-scatter.2.cloned.1.call-start = ((), (), s32[]{:S(2)}) async-start(), calls=%async_computation.3 | async-start | bytes 3538944 | tf_op jit(solution)/shard_map/reduce_scatter | solution.py:157
  394.9 49.0 %copy-start.2 = (bf16[384,384]{1,0:T(8,128)(2,1)S(1)}, bf16[384,384]{1,0:T(8,128)(2,1)}, u32[]{:S(2)}) copy-start(bf16[384,384]{1,0:T(8,128)(2,1)} %param.13) | copy-start | bytes 884740
  394.9 49.8 %copy-start.1 = (f32[128,768]{1,0:T(8,128)S(1)}, f32[128,768]{1,0:T(8,128)}, u32[]{:S(2)}) copy-start(f32[128,768]{1,0:T(8,128)} %param.15) | copy-start | bytes 1179652
Sparse Core Ops, SparseCore 0:
  12.4 134.4 all-gather.8
  151.4 156.5 all-gather.6
  310.1 72.6 all-gather.4
  395.1 47.6 reduce-scatter.1

commit v2 on v0

v2 whole, which is shorter than its diff:
```python
import math

import jax
import jax.numpy as jnp
from jax import lax
from jax.experimental import pallas as pl
from jax.experimental.pallas import tpu as pltpu
from jax.sharding import PartitionSpec as P

MESH = pl.DeviceIdType.MESH


def position():
    w = lax.axis_index("wide")
    n = lax.axis_index("narrow")
    return w // 8, (w // 2) % 4, (w % 2) * 4 + n // 2, n % 2


def device(y, x, z, c):
    return ((y * 4 + x) * 2 + z // 4, (z % 4) * 2 + c)


CHUNKS = 4
ROWS = 128 // CHUNKS
WIDTH = 896
SLOTS = 320
LEAD = 2
Z, O, PW, PD, CTX, PICK, UNIT, PROJ, PAIR, P1, P2, FIN, UP, DOWN, GRAD = range(15)
FAR_FIRST = (4, 3, 5, 2, 6, 1, 7)
NEAR_FIRST = (1, 7, 2, 6, 3, 5, 4)
TOKENS = 65536
PLANES = ((0, 1), (-1, 2), (-2, 3), (-3, 4))
SPAN = {O: (0, 64), PW: (0, 48), PD: (48, 16)}
ORDER = (
    (O, 0, 0, 1, 0), (O, 0, 0, 1, 1), (O, 1, 0, 1, 0), (O, 1, 0, 1, 1), (CTX, 0, 0, 0), (CTX, 1, 0, 0),
    (O, 0, 0, 2, 0), (O, 0, 0, 2, 1), (O, 1, 0, 2, 0), (Z,), (O, 1, 0, 2, 1), (O, 0, -1, 1, 0), (O, 0, -1, 1, 1),
    (CTX, 0, 1, 0), (CTX, 1, 1, 0), (O, 0, 1, 1, 0), (O, 0, 1, 1, 1), (PW, 1, 0, 1, 1), (O, 1, 0, 3, 0),
    (PD, 1, 0, 1, 1), (O, 0, -2, 1, 0), (O, 0, -2, 1, 1), (PW, 1, 0, 1, 0), (PD, 1, 0, 1, 0), (O, 1, 0, 3, 1),
    (CTX, 0, 0, 1), (CTX, 1, 0, 1), (PW, 0, 0, 1, 0), (PW, 0, 0, 1, 1), (PD, 0, 0, 1, 0), (O, 1, 0, 4, 0),
    (PD, 0, 0, 1, 1), (PW, 1, 0, 2, 1), (PD, 1, 0, 2, 1), (PW, 1, 0, 2, 0), (O, 0, 2, 1, 0), (O, 0, 2, 1, 1),
    (O, 1, 0, 4, 1), (PD, 1, 0, 2, 0), (O, 0, -1, 2, 0), (O, 0, -1, 2, 1), (CTX, 0, 2, 0), (CTX, 1, 2, 0),
    (PW, 1, -1, 1, 1), (PW, 1, -1, 1, 0), (O, 0, 1, 2, 0), (O, 0, 1, 2, 1), (PW, 1, 1, 1, 1), (PW, 1, 1, 1, 0),
    (O, 0, -3, 1, 0), (O, 0, -3, 1, 1), (PD, 0, 1, 1, 0), (PD, 0, 1, 1, 1), (PW, 1, 0, 3, 1), (PW, 1, 0, 3, 0),
    (PD, 1, 0, 3, 1), (CTX, 0, 1, 1), (CTX, 1, 1, 1), (PD, 1, 0, 3, 0), (O, 0, -2, 2, 0), (O, 0, -2, 2, 1),
    (PD, 0, -1, 1, 0), (PD, 0, -1, 1, 1), (PW, 1, -1, 2, 1), (PW, 1, -1, 2, 0), (O, 0, 3, 1, 0), (O, 0, 3, 1, 1),
    (PW, 1, 1, 2, 1), (PW, 1, 1, 2, 0), (PW, 0, 0, 2, 1), (PW, 1, 0, 4, 1), (PW, 0, 0, 2, 0), (PD, 0, 2, 1, 1),
    (CTX, 0, 3, 0), (CTX, 1, 3, 0), (PW, 1, 0, 4, 0), (PD, 0, 0, 2, 0), (PD, 1, 0, 4, 0), (PD, 0, 2, 1, 0),
    (O, 0, 2, 2, 1), (PW, 1, -1, 3, 1), (PICK, 0), (O, 0, 2, 2, 0), (PW, 1, -1, 3, 0), (PW, 1, 1, 3, 1),
    (O, 0, 4, 1, 1), (PD, 0, -2, 1, 1), (PW, 1, 1, 3, 0), (O, 0, 4, 1, 0), (PW, 1, 2, 1, 1), (CTX, 0, 0, 2),
    (CTX, 1, 0, 2), (PD, 0, -2, 1, 0), (O, 0, -3, 2, 1), (PD, 0, 1, 2, 1), (PW, 1, -1, 4, 1), (PW, 1, 2, 1, 0),
    (O, 0, -3, 2, 0), (PD, 0, 3, 1, 1), (PW, 1, -1, 4, 0), (PD, 0, 3, 1, 0), (PD, 0, -3, 1, 1), (PW, 1, 1, 4, 1),
    (PW, 1, 1, 4, 0), (PD, 0, -3, 1, 0), (PD, 0, -1, 2, 1), (PICK, 1), (PICK, -1), (UNIT, 0, 0), (O, 0, 3, 2, 0),
    (O, 0, 3, 2, 1), (PW, 1, 2, 2, 1), (PD, 0, 4, 1, 0), (PD, 0, 4, 1, 1), (CTX, 0, 2, 1), (CTX, 1, 2, 1),
    (PD, 0, 2, 2, 0), (PW, 1, 2, 2, 0), (PICK, 2), (UNIT, 1, 0), (O, 0, 4, 2, 1), (O, 0, 4, 2, 0), (PD, 0, 3, 2, 1),
    (PD, 0, -2, 2, 0), (PD, 0, -3, 2, 1), (PICK, 3), (PD, 0, 4, 2, 0), (PICK, -2), (PICK, -3), (PICK, 4),
    (PW, 1, 2, 3, 1), (UNIT, 2, 0), (PW, 1, 2, 3, 0), (CTX, 0, 1, 2), (CTX, 1, 1, 2), (PW, 1, 2, 4, 1), (UNIT, 0, 1),
    (PW, 1, 2, 4, 0), (UNIT, 3, 0), (PROJ, 0), (CTX, 0, 3, 1), (CTX, 1, 3, 1), (UNIT, 1, 1), (UNIT, 2, 1),
    (UNIT, 3, 1), (PAIR, 0), (PROJ, 1), (CTX, 0, 2, 2), (CTX, 1, 2, 2), (PAIR, 1), (P1, 0, 0), (UNIT, 0, 2),
    (CTX, 0, 3, 2), (CTX, 1, 3, 2), (UNIT, 1, 2), (UNIT, 2, 2), (P1, 0, 1), (UNIT, 3, 2), (PROJ, 2), (P2, 0),
    (UNIT, 0, 3), (UNIT, 1, 3), (UNIT, 2, 3), (UNIT, 3, 3), (PAIR, 2), (P1, 1, 0), (PROJ, 3), (FIN, 0), (P1, 1, 1),
    (PAIR, 3), (P2, 1), (P1, 2, 0), (P1, 2, 1), (FIN, 1), (P2, 2), (P1, 3, 0), (FIN, 2), (P1, 3, 1), (P2, 3),
    (FIN, 3),
)


def half(kind, side, flip):
    if kind == O:
        return (32 * side, 32)
    if kind == PW:
        return ((0, 32), (32, 16))[side] if flip == 0 else ((0, 16), (16, 32))[side]
    return (48, 16) if side == flip else None


def split(value):
    high = value.astype(jnp.bfloat16)
    rest = value - high.astype(jnp.float32)
    middle = rest.astype(jnp.bfloat16)
    low = (rest - middle.astype(jnp.float32)).astype(jnp.bfloat16)
    return high, middle, low


def exact_dot(value, weight, contract):
    rows = value.shape[0]
    tall = lax.dot_general(
        jnp.concatenate(split(value), axis=0), weight, (((1,), (contract,)), ((), ())), preferred_element_type=jnp.float32
    )
    return (tall[2 * rows:] + tall[rows:2 * rows]) + tall[:rows]


def gelu_and_slope(v):
    scale = math.sqrt(2.0 / math.pi)
    square = v * v
    bent = jnp.tanh(scale * (v + 0.044715 * (square * v)))
    share = 0.5 * (1.0 + bent)
    slope = share + 0.5 * v * (1.0 - bent * bent) * (scale * (1.0 + 3.0 * 0.044715 * square))
    return v * share, slope


def fused_kernel(
    ctx_ref, weight_ref, side_ref, gain_ref, res_hbm, f_hbm, g_hbm, targets_hbm, o_ref, f_out, g_out,
    pack_ref, res_ref, f_ref, g_ref, targets_ref, wbuf, cbuf, down, acc, part, pair, line, up_in, down_in, sums,
    grads, buf0, summed, buf_a, mid, buf_b, buf_x, tail, fin, local, send_sems, recv_sems
):
    y, x, z, c = position()
    j = z % 4
    n = j * 2 + c
    zh = z // 4
    sibling = device(y, x, z, 1 - c)
    y_dev = (device((y + 1) % 8, x, z, c), device((y + 7) % 8, x, z, c))
    x_dev = (device(y, (x + 1) % 4, z, c), device(y, (x + 3) % 4, z, c))
    z_dev = (device(y, x, (z + 1) % 8, c), device(y, x, (z + 7) % 8, c))
    z_far = device(y, x, (z + 4) % 8, c)

    on_z = 1 - c
    pos_a = z * on_z + y * c
    pos_b = y * on_z + z * c

    def along_a(d):
        return device((y + d * c) % 8, x, (z + d * on_z) % 8, c)

    def along_b(d):
        return device((y + d * on_z) % 8, x, (z + d * c) % 8, c)

    def along_x(d):
        return device(y, (x + d) % 4, z, c)

    barrier = pltpu.get_barrier_semaphore()
    partners = [sibling]
    partners += [along_a(d) for d in range(1, 8)] + [along_b(d) for d in range(1, 8)] + [along_x(d) for d in range(1, 4)]
    for partner in partners:
        pl.semaphore_signal(barrier, inc=1, device_id=partner, device_id_type=MESH)
    loads = [
        pltpu.make_async_copy(src, dst, local.at[2 + i])
        for i, (src, dst) in enumerate(
            ((res_hbm, res_ref), (f_hbm, f_ref), (g_hbm, g_ref), (targets_hbm, targets_ref))
        )
    ]
    for load in loads:
        load.start()
    pack_ref[0:48, :] = weight_ref[...]
    pack_ref[48:64, :] = jnp.zeros((16, 768), jnp.bfloat16)
    pack_ref[48:60, :] = side_ref[...]
    pl.semaphore_wait(barrier, len(partners))

    slots = {}
    sent = []
    begun = set()

    def remote(key, src, dst, to):
        at = slots.setdefault(key, len(slots))
        return pltpu.make_async_remote_copy(
            src_ref=src, dst_ref=dst, send_sem=send_sems.at[at], recv_sem=recv_sems.at[at], device_id=to, device_id_type=MESH
        )

    def only(chips, action):
        if chips is None:
            action()
            return
        for chip in chips:
            pl.when(j == chip)(action)

    def send(key, make, chips=None):
        only(chips, lambda: remote(key, *make()).start())
        sent.append((key, make, chips))

    def wait(key, region):
        remote(key, region, region, sibling).wait_recv()

    def plane(dy):
        return (y + dy + 8) % 8

    def block(kind, dy, dx, span=None):
        start, count = span or SPAN[kind]
        side = zh if kind == O else 1 - zh
        at = (plane(dy) * 4 + (x + dx + 4) % 4) * 2 + side
        return wbuf.at[at, pl.ds(start, count)]

    def send_block(key, kind, dy, dx, to, span=None):
        if kind == O and dy == 0 and dx == 0:
            send(key, lambda: (pack_ref, block(O, 0, 0), to))
        else:
            send(key, lambda: (block(kind, dy, dx, span), block(kind, dy, dx, span), to))

    def start_x(kind, dy):
        for s in (0, 1):
            send_block((kind, 0, dy, 1, s), kind, dy, 0, x_dev[s])

    def start_y(q):
        for s in (0, 1):
            send_block((PW, 1, q, 1, s), PW, 0, q, y_dev[s])

    def lanes(t, index):
        return cbuf.at[:, pl.ds(t * ROWS, ROWS), pl.ds(pl.multiple_of(index * 384, 128), 384)]

    def mine(t):
        return ctx_ref.at[:, pl.ds(t * ROWS, ROWS), :]

    def own_ctx(t, side, chips):
        send((CTX, side, t, 0), lambda: (mine(t), lanes(t, n), z_dev[side]), chips)

    def after_both(key):
        twin = key[:-1] + (1 - key[-1],)
        begun.add(key)
        return twin in begun

    def z_event(key):
        wait(key, wbuf.at[(y * 4 + x) * 2 + 1 - zh])
        for s in (0, 1):
            send_block((PW, 0, 0, 1, s), PW, 0, 0, x_dev[s])
        start_y(0)
        for s in (0, 1):
            send_block((PD, 1, 0, 1, s), PD, 0, 0, y_dev[s])
        start_x(PD, 0)

    def y_first(key):
        kind, _, _, s, side = key
        dy = (-1 if side == 0 else 1) * s
        wait(key, block(kind, dy, 0, half(kind, side, 0) if s == 4 else None))
        if s < 4:
            span = half(kind, side, 0) if s == 3 else SPAN[kind]
            if span:
                send_block((kind, 1, 0, s + 1, side), kind, dy, 0, y_dev[side], span)
            start_x(kind, dy)
        elif kind == PD or after_both(key):
            start_x(kind, 4)

    def x_second(key):
        kind, _, dy, s, side = key
        dx = (-1 if side == 0 else 1) * s
        span = half(kind, side, dy % 2)
        wait(key, block(kind, dy, dx, span if s == 2 else None))
        if s == 1 and span:
            send_block((kind, 0, dy, 2, side), kind, dy, dx, x_dev[side], span)

    def x_first(key):
        _, _, _, s, side = key
        dx = (-1 if side == 0 else 1) * s
        span = half(PW, side, 0)
        wait(key, block(PW, 0, dx, span if s == 2 else None))
        if s == 1:
            send_block((PW, 0, 0, 2, side), PW, 0, dx, x_dev[side], span)
            start_y(dx)
        elif after_both(key):
            start_y(2)

    def y_second(key):
        _, _, q, s, side = key
        dy = (-1 if side == 0 else 1) * s
        span = half(PW, side, q % 2)
        wait(key, block(PW, dy, q, span if s == 4 else None))
        if s < 4:
            send_block((PW, 1, q, s + 1, side), PW, dy, q, y_dev[side], span if s == 3 else None)

    def reach(side, h):
        return range(1 + h, 4) if side == 0 else range(0, 3 - h)

    def source(side, h):
        return j + (-1 if side == 0 else 1) * (1 + h)

    def ctx_event(key):
        _, side, t, h = key
        chips = reach(side, h)
        region = lambda: lanes(t, source(side, h) * 2 + c)
        onward = [k for k in chips if (k < 3 if side == 0 else k > 0)]
        only(chips, lambda: wait(key, region()))
        if onward:
            send((CTX, side, t, h + 1), lambda: (region(), region(), z_dev[side]), onward)
        send((CTX, side + 2, t, h), lambda: (region(), region(), sibling), chips)
        if h == 0 and t + LEAD < CHUNKS:
            own_ctx(t + LEAD, side, (1, 2))

    def keep():
        return pltpu.make_async_copy(pack_ref, block(O, 0, 0), local.at[0]), pltpu.make_async_copy(
            ctx_ref, cbuf.at[:, :, pl.ds(pl.multiple_of(n * 384, 128), 384)], local.at[1]
        )

    def pick(key):
        if PICK not in begun:
            begun.add(PICK)
            for copy in keep():
                copy.wait()
        lane = lax.broadcasted_iota(jnp.int32, (96, 128), 1)
        row = lax.broadcasted_iota(jnp.int32, (96, 128), 0)
        here = ((lane & 15) < 12) & ((lane >> 4) * 12 + (lane & 15) == row)
        chosen = jnp.where(here, 1.0, 0.0).astype(jnp.bfloat16)
        k = plane(key[1])
        padded = wbuf[pl.ds(pl.multiple_of(k * 8, 8), 8), 48:64, :].reshape(128, 768)
        picked = jnp.dot(chosen, padded, preferred_element_type=jnp.float32)
        down[pl.ds(pl.multiple_of(k * 96, 32), 96), :] = picked.astype(jnp.bfloat16)

    def unit(key):
        _, p, t = key
        if (CTX, t) not in begun:
            begun.add((CTX, t))
            for h in range(3):
                for side in (0, 1):
                    only(reach(side, h), lambda: wait((CTX, side + 2, t, h), lanes(t, source(side, h) * 2 + 1 - c)))
            wait((CTX, 4, t, 0), lanes(t, j * 2 + 1 - c))
        here = pl.ds(t * ROWS, ROWS)
        ks = [plane(dy) for dy in PLANES[p]]
        lhs = [cbuf[:, here, pl.ds(pl.multiple_of(k * 384, 128), 384)].reshape(8 * ROWS, 384) for k in ks]
        rhs = [wbuf[pl.ds(pl.multiple_of(k * 8, 8), 8), 0:48, :].reshape(384, 768) for k in ks]
        product = jnp.dot(
            jnp.concatenate(lhs, axis=1), jnp.concatenate(rhs, axis=0), preferred_element_type=jnp.float32
        )
        if (UNIT, t) in begun:
            acc[t] += product
        else:
            begun.add((UNIT, t))
            acc[t] = product

    def project(key):
        t = key[1]
        here = pl.ds(t * ROWS, ROWS)
        if PROJ not in begun:
            begun.add(PROJ)
            loads[0].wait()
        gain = gain_ref[...].astype(jnp.float32)
        stream = (res_ref[:, here, :].reshape(8 * ROWS, 768).astype(jnp.float32) + acc[t]).astype(jnp.bfloat16)
        value = stream.astype(jnp.float32)
        total = jnp.sum(value, axis=1, keepdims=True)
        squares = jnp.sum(value * value, axis=1, keepdims=True)
        scaled = (value * gain).astype(jnp.bfloat16)
        mapped = lax.dot_general(scaled, down[...], (((1,), (1,)), ((), ())), preferred_element_type=jnp.float32)
        column = lax.broadcasted_iota(jnp.int32, (8 * ROWS, 128), 1)
        stats = jnp.where(column == 0, total, jnp.where(column == 1, squares, 0.0))
        for k in range(8):
            cut = slice(k * ROWS, (k + 1) * ROWS)
            part[t, k % 2, k // 2, 0:ROWS, 0:768] = mapped[cut]
            part[t, k % 2, k // 2, 0:ROWS, 768:896] = stats[cut]
        if t == 0:
            rows = jnp.broadcast_to(gain, (16, 768)).astype(jnp.bfloat16)
            gain_rows = lax.dot_general(rows, down[...], (((1,), (1,)), ((), ())), preferred_element_type=jnp.float32)
            for k in range(8):
                part[0, k % 2, k // 2, ROWS:ROWS + 8, 0:768] = gain_rows[0:8]
                part[0, k % 2, k // 2, ROWS:ROWS + 8, 768:896] = jnp.zeros((8, 128), jnp.float32)
        rows_sent = pl.ds(0, tall(t))
        send((PAIR, t), lambda: (part.at[t, 1 - c, :, rows_sent], pair.at[t, :, rows_sent], sibling))

    def tall(t):
        return ROWS + 8 if t == 0 else ROWS

    def piece(ref, t, dest):
        return ref.at[t, dest, pl.ds(0, tall(t))]

    def add_pair(key):
        t = key[1]
        rows = pl.ds(0, tall(t))
        wait(key, pair.at[t, :, rows])
        line[t, :, rows] = part[t, c, :, rows] + pair[t, :, rows]
        for i in range(3):
            pass_on(t, 0, 0, 3 - i, True)
            pass_on(t, 3, 1, i, True)

    def pass_on(t, chip, side, dest, first=False):
        kind, arrived = ((UP, up_in), (DOWN, down_in))[side]
        if not first:

            def add():
                wait((kind, t, dest), piece(arrived, t, dest))
                line[t, dest, 0:tall(t)] += arrived[t, dest, 0:tall(t)]

            only((chip,), add)
        send((kind, t, dest), lambda: (piece(line, t, dest), piece(arrived, t, dest), z_dev[side]), (chip,))

    def finish(key):
        t = key[1]
        for chip in range(4):

            def add():
                total = line[t, chip, 0:tall(t)]
                if chip > 0:
                    wait((UP, t, chip), piece(up_in, t, chip))
                    total = total + up_in[t, chip, 0:tall(t)]
                if chip < 3:
                    wait((DOWN, t, chip), piece(down_in, t, chip))
                    total = total + down_in[t, chip, 0:tall(t)]
                sums[t * ROWS:(t + 1) * ROWS, :] = total[0:ROWS]
                if t == 0:
                    sums[128:136, :] = total[ROWS:ROWS + 8]

            only((chip,), add)

    def task(key):
        kind = key[0]
        if kind == Z:
            z_event(key)
        elif kind in (O, PD):
            (y_first if key[1] else x_second)(key)
        elif kind == PW:
            (y_second if key[1] else x_first)(key)
        elif kind == CTX:
            ctx_event(key)
        elif kind == P1:
            _, t, i = key
            pass_on(t, 1, 0, 3 - i)
            pass_on(t, 2, 1, i)
        elif kind == P2:
            pass_on(key[1], 2, 0, 3)
            pass_on(key[1], 1, 1, 0)
        else:
            {PICK: pick, UNIT: unit, PROJ: project, PAIR: add_pair, FIN: finish}[kind](key)

    def side_block():
        for load in loads[1:]:
            load.wait()
        mean = sums[0:128, 768:769] * (1.0 / (8 * 768))
        spread = sums[0:128, 769:770] * (1.0 / (8 * 768)) - mean * mean
        scale = 1.0 / jnp.sqrt(spread + 1e-06)
        first = (sums[0:128, 0:384] - mean * sums[128:129, 0:384]) * scale
        second = (sums[0:128, 384:768] - mean * sums[128:129, 384:768]) * scale
        bend, f_slope = gelu_and_slope(exact_dot(second, f_ref[...], 0))
        upper = first + bend
        bend, g_slope = gelu_and_slope(exact_dot(upper, g_ref[...], 0))
        lower = second + bend
        o_ref[:, 0:384] = upper
        o_ref[:, 384:768] = lower
        back = (lower - targets_ref[:, 384:768]) * (1.0 / TOKENS) * g_slope
        upper_total = (upper - targets_ref[:, 0:384]) * (1.0 / TOKENS) + exact_dot(back, g_ref[...], 1)
        whole = lax.Precision.HIGHEST
        over_tokens = (((0,), (0,)), ((), ()))
        grads[1] = lax.dot_general(upper, back, over_tokens, precision=whole, preferred_element_type=jnp.float32)
        grads[0] = lax.dot_general(second, upper_total * f_slope, over_tokens, precision=whole, preferred_element_type=jnp.float32)

    def rows_of(ref, at, count):
        return ref.at[pl.ds(pl.multiple_of(at * count, 8), count)]

    def gradient_sum():
        send((GRAD, 0), lambda: (grads.at[1 - c], buf0, sibling))
        wait((GRAD, 0), buf0)
        summed[...] = grads[c] + buf0[...]
        for d in FAR_FIRST:
            send((GRAD, d), lambda d=d: (rows_of(summed, (pos_a + d) % 8, 48), buf_a.at[d - 1], along_a(d)))
        total = summed[pl.ds(pl.multiple_of(pos_a * 48, 8), 48), :]
        for d in FAR_FIRST:
            wait((GRAD, d), buf_a.at[d - 1])
            total = total + buf_a[d - 1]
        mid[0:48, :] = total
        mid[48:64, :] = jnp.zeros((16, 384), jnp.float32)
        for d in FAR_FIRST:
            send((GRAD, 7 + d), lambda d=d: (rows_of(mid, (pos_b + d) % 8, 8), buf_b.at[d - 1], along_b(d)))
        total = mid[pl.ds(pl.multiple_of(pos_b * 8, 8), 8), :]
        for d in FAR_FIRST:
            wait((GRAD, 7 + d), buf_b.at[d - 1])
            total = total + buf_b[d - 1]
        buf_x[x] = total
        for d in (2, 1, 3):
            send((GRAD, 14 + d), lambda d=d: (buf_x.at[x], buf_x.at[x], along_x(d)))
        for d in (2, 1, 3):
            wait((GRAD, 14 + d), buf_x.at[(x + 4 - d) % 4])
        tail[pl.ds(pl.multiple_of(pos_b * 8, 8), 8), :] = (buf_x[0] + buf_x[1]) + (buf_x[2] + buf_x[3])
        for d in FAR_FIRST:
            send((GRAD, 17 + d), lambda d=d: (rows_of(tail, pos_b, 8), rows_of(tail, pos_b, 8), along_b(d)))
        for d in FAR_FIRST:
            wait((GRAD, 17 + d), rows_of(tail, (pos_b + 8 - d) % 8, 8))
        for d in FAR_FIRST:
            send((GRAD, 24 + d), lambda d=d: (tail.at[pl.ds(0, 48)], fin.at[c, pl.ds(pl.multiple_of(pos_a * 48, 8), 48)], along_a(d)))
        send((GRAD, 32), lambda: (tail.at[pl.ds(0, 48)], fin.at[c, pl.ds(pl.multiple_of(pos_a * 48, 8), 48)], sibling))
        fin[c, pl.ds(pl.multiple_of(pos_a * 48, 8), 48), :] = tail[0:48, :]

        def there(d, core, far):
            base = far * y + (1 - far) * z
            return fin.at[core, pl.ds(pl.multiple_of((base + 8 - d) % 8 * 48, 8), 48)]

        for d in NEAR_FIRST:
            wait((GRAD, 24 + d), there(d, c, c))
            send((GRAD, 32 + d), lambda d=d: (there(d, c, c), there(d, c, c), sibling))
        wait((GRAD, 32), there(0, 1 - c, 1 - c))
        for d in NEAR_FIRST:
            wait((GRAD, 32 + d), there(d, 1 - c, 1 - c))
        f_out[...] = fin[0]
        g_out[...] = fin[1]

    send((Z,), lambda: (pack_ref, block(O, 0, 0), z_far))
    for s in (0, 1):
        send_block((O, 1, 0, 1, s), O, 0, 0, y_dev[s])
    start_x(O, 0)
    for t in range(CHUNKS):
        own_ctx(t, 0, (0, 1, 2) if t < LEAD else (0,))
        own_ctx(t, 1, (1, 2, 3) if t < LEAD else (3,))
    for t in range(CHUNKS):
        send((CTX, 4, t, 0), lambda t=t: (mine(t), lanes(t, n), sibling))
    for copy in keep():
        copy.start()
    for key in ORDER:
        task(key)
    side_block()
    gradient_sum()
    for key, make, chips in sent:
        only(chips, lambda: remote(key, *make()).wait_send())


def fused(context, out_weight, side_down, ln_gain, residual, f_weight, g_weight, targets):
    vmem = pl.BlockSpec(memory_space=pltpu.VMEM)
    away = pl.BlockSpec(memory_space=pl.ANY)
    tall = ROWS + 8
    f32 = jnp.float32
    bf16 = jnp.bfloat16
    piece = pltpu.VMEM((CHUNKS, 4, tall, WIDTH), f32)
    square = jax.ShapeDtypeStruct((384, 384), f32)
    return pl.pallas_call(
        fused_kernel,
        out_shape=(jax.ShapeDtypeStruct((128, 768), f32), square, square),
        in_specs=[vmem] * 4 + [away] * 4,
        out_specs=(vmem, vmem, vmem),
        scratch_shapes=[
            pltpu.VMEM((64, 768), bf16),
            pltpu.VMEM((8, 128, 768), bf16),
            pltpu.VMEM((384, 384), bf16),
            pltpu.VMEM((384, 384), bf16),
            pltpu.VMEM((128, 768), f32),
            pltpu.VMEM((64, 64, 768), bf16),
            pltpu.VMEM((8, 128, 3072), bf16),
            pltpu.VMEM((768, 768), bf16),
            pltpu.VMEM((CHUNKS, 8 * ROWS, 768), f32),
            pltpu.VMEM((CHUNKS, 2, 4, tall, WIDTH), f32),
            piece,
            piece,
            piece,
            piece,
            pltpu.VMEM((136, WIDTH), f32),
            pltpu.VMEM((2, 384, 384), f32),
            pltpu.VMEM((384, 384), f32),
            pltpu.VMEM((384, 384), f32),
            pltpu.VMEM((7, 48, 384), f32),
            pltpu.VMEM((64, 384), f32),
            pltpu.VMEM((7, 8, 384), f32),
            pltpu.VMEM((4, 8, 384), f32),
            pltpu.VMEM((64, 384), f32),
            pltpu.VMEM((2, 384, 384), f32),
            pltpu.SemaphoreType.DMA((6,)),
            pltpu.SemaphoreType.DMA((SLOTS,)),
            pltpu.SemaphoreType.DMA((SLOTS,)),
        ],
        compiler_params=pltpu.CompilerParams(collective_id=0, has_side_effects=True, vmem_limit_bytes=60 * 1024 * 1024),
        name="fused_layer",
    )(
        context.reshape(8, 128, 384), out_weight, side_down.T, ln_gain.reshape(1, 768), residual.reshape(8, 128, 768),
        f_weight, g_weight, targets,
    )


def per_device(context, out_weight, residual, ln_gain, side_down, f_weight, g_weight, targets):
    return fused(context, out_weight, side_down, ln_gain, residual, f_weight, g_weight, targets)


def solution(mesh):
    in_specs = (
        P("wide", "narrow"),
        P("wide", "narrow"),
        P("wide", "narrow"),
        P("narrow"),
        P("narrow", "wide"),
        P(),
        P(),
        P(("wide", "narrow"), None),
    )
    out_specs = (P(("wide", "narrow"), None), P(), P())
    return jax.shard_map(
        per_device, mesh=mesh, in_specs=in_specs, out_specs=out_specs, check_vma=False
    )
```

time: 739 us -> 153 us (0.21)
  waiting for transfers between devices: 672 us -> 0 us
  Pallas kernels: 0 us -> 146 us
  blocking collectives: 25.3 us -> 0 us
  matrix products: 17.4 us -> 0 us
  between operations: 13.9 us -> 0.65 us
    all_gather x3 -> x0, waiting for transfers between devices: 369 us -> none  [the longest x1 159 us: per_device(): full_weight = lax.all_gather(out_weight, 'wide', axis=0, tiled=True)]
    psum x1 -> x0, waiting for transfers between devices: 279 us -> none  [per_device(): f_total, g_total = lax.psum((f_local, g_local), ('wide', 'narrow'))]
    pallas_call x0 -> x1, Pallas kernels: none -> 146 us  [fused(): pl.pallas_call(fused_kernel, out_shape=(jax.ShapeDtypeStruct((128, 768),...]
    psum x1 -> x0, blocking collectives: 25.3 us -> none  [per_device(): lax.psum((row_sum, row_squares, gain_part), 'narrow')]
    reduce_scatter x1 -> x0, waiting for transfers between devices: 22 us -> none  [per_device(): lax.psum_scatter(jnp.dot(scaled, down_full, preferred_element_type=jnp.fl...]
    dot_general x9 -> x0, matrix products: 17.4 us -> none  [the longest x1 8.86 us: per_device(): attn_sum = jnp.dot(whole, full_weight, preferred_element_type=jnp.float32)]
  transfers between devices with their start and end apart: 5 -> 0, of which waited for: 5 -> 0; matrix products, arithmetic and copies ran while one was open for 1% -> 0% of each run, Pallas kernels for 0% -> 0%
where the time goes in v2:
time: 153 us
  Pallas kernels  146 us (95%)
  local copies, waits for them, and re-layouts  5.83 us (4%)
    pallas_call x1, Pallas kernels, fused(): pl.pallas_call(fused_kernel, out_shape=(jax.ShapeDtypeStruct((128, 768),...  146 us
    unnamed x5, local copies, waits for them, and re-layouts  4.56 us

profile of v2, /device:TPU:1, one launch (start us, length us, event | category | flops | bytes accessed | tf_op | source)
XLA Modules:
  0.0 152.6 jit_solution(24886693653420608)
XLA Ops:
  0.6 1.3 reshape.16.gain_ref
  1.9 146.1 %fused_layer.1 = (f32[128,768]{1,0:T(8,128)}, f32[384,384]{1,0:T(8,128)}, f32[384,384]{1,0:T(8,128)}) custom-call(bf16[8,128,384]{2,1,0:T(8,128)(2,1)} %bitcast.4, bf16[48,768]{1,0:T(8,128)(2,1)} %weight_ref.1, bf16[12,768]{1,0:T(8,128)(2,1)} %bitcast.5, bf16[1,768]{1,0:T(2,128)(2,1)} %reshape.16.gain_ref, bf16[8,128,768]{2,1,0:T(8,128)(2,1)} %bitcast.3, ...), custom_call_target="tpu_custom_call" | custom-call | tf_op jit(solution)/shard_map/fused_layer/pallas_call | solution.py:501
  148.0 0.0 copy-start
  148.0 1.8 %copy.14 = f32[128,768]{1,0:T(8,128)} copy(f32[128,768]{1,0:T(8,128)} %get-tuple-element.6) | data formatting | bytes 786432
  149.9 1.9 %copy.15 = f32[384,384]{1,0:T(8,128)} copy(f32[384,384]{1,0:T(8,128)} %get-tuple-element.7) | data formatting | bytes 1179648
  151.8 0.0 copy-done
  151.8 0.8 copy.16
Async XLA Ops:
  148.0 3.8 %copy-start = (f32[384,384]{1,0:T(8,128)S(1)}, f32[384,384]{1,0:T(8,128)}, u32[]{:S(2)}) copy-start(f32[384,384]{1,0:T(8,128)} %get-tuple-element.8) | copy-start | bytes 1769476

commit v3 on v2

--- a/solution.py
+++ b/solution.py
@@ -22,10 +22,10 @@
 
 CHUNKS = 4
 ROWS = 128 // CHUNKS
-WIDTH = 896
+WIDTH = 768
 SLOTS = 320
 LEAD = 2
-Z, O, PW, PD, CTX, PICK, UNIT, PROJ, PAIR, P1, P2, FIN, UP, DOWN, GRAD = range(15)
+Z, O, PW, PD, CTX, PICK, UNIT, PROJ, PAIR, P1, P2, FIN, UP, DOWN, GRAD, STAT = range(16)
 FAR_FIRST = (4, 3, 5, 2, 6, 1, 7)
 NEAR_FIRST = (1, 7, 2, 6, 3, 5, 4)
 TOKENS = 65536
@@ -35,31 +35,31 @@
     (O, 0, 0, 1, 0), (O, 0, 0, 1, 1), (O, 1, 0, 1, 0), (O, 1, 0, 1, 1), (CTX, 0, 0, 0), (CTX, 1, 0, 0),
     (O, 0, 0, 2, 0), (O, 0, 0, 2, 1), (O, 1, 0, 2, 0), (Z,), (O, 1, 0, 2, 1), (O, 0, -1, 1, 0), (O, 0, -1, 1, 1),
     (CTX, 0, 1, 0), (CTX, 1, 1, 0), (O, 0, 1, 1, 0), (O, 0, 1, 1, 1), (PW, 1, 0, 1, 1), (O, 1, 0, 3, 0),
-    (PD, 1, 0, 1, 1), (O, 0, -2, 1, 0), (O, 0, -2, 1, 1), (PW, 1, 0, 1, 0), (PD, 1, 0, 1, 0), (O, 1, 0, 3, 1),
-    (CTX, 0, 0, 1), (CTX, 1, 0, 1), (PW, 0, 0, 1, 0), (PW, 0, 0, 1, 1), (PD, 0, 0, 1, 0), (O, 1, 0, 4, 0),
-    (PD, 0, 0, 1, 1), (PW, 1, 0, 2, 1), (PD, 1, 0, 2, 1), (PW, 1, 0, 2, 0), (O, 0, 2, 1, 0), (O, 0, 2, 1, 1),
-    (O, 1, 0, 4, 1), (PD, 1, 0, 2, 0), (O, 0, -1, 2, 0), (O, 0, -1, 2, 1), (CTX, 0, 2, 0), (CTX, 1, 2, 0),
-    (PW, 1, -1, 1, 1), (PW, 1, -1, 1, 0), (O, 0, 1, 2, 0), (O, 0, 1, 2, 1), (PW, 1, 1, 1, 1), (PW, 1, 1, 1, 0),
-    (O, 0, -3, 1, 0), (O, 0, -3, 1, 1), (PD, 0, 1, 1, 0), (PD, 0, 1, 1, 1), (PW, 1, 0, 3, 1), (PW, 1, 0, 3, 0),
-    (PD, 1, 0, 3, 1), (CTX, 0, 1, 1), (CTX, 1, 1, 1), (PD, 1, 0, 3, 0), (O, 0, -2, 2, 0), (O, 0, -2, 2, 1),
-    (PD, 0, -1, 1, 0), (PD, 0, -1, 1, 1), (PW, 1, -1, 2, 1), (PW, 1, -1, 2, 0), (O, 0, 3, 1, 0), (O, 0, 3, 1, 1),
-    (PW, 1, 1, 2, 1), (PW, 1, 1, 2, 0), (PW, 0, 0, 2, 1), (PW, 1, 0, 4, 1), (PW, 0, 0, 2, 0), (PD, 0, 2, 1, 1),
-    (CTX, 0, 3, 0), (CTX, 1, 3, 0), (PW, 1, 0, 4, 0), (PD, 0, 0, 2, 0), (PD, 1, 0, 4, 0), (PD, 0, 2, 1, 0),
-    (O, 0, 2, 2, 1), (PW, 1, -1, 3, 1), (PICK, 0), (O, 0, 2, 2, 0), (PW, 1, -1, 3, 0), (PW, 1, 1, 3, 1),
-    (O, 0, 4, 1, 1), (PD, 0, -2, 1, 1), (PW, 1, 1, 3, 0), (O, 0, 4, 1, 0), (PW, 1, 2, 1, 1), (CTX, 0, 0, 2),
-    (CTX, 1, 0, 2), (PD, 0, -2, 1, 0), (O, 0, -3, 2, 1), (PD, 0, 1, 2, 1), (PW, 1, -1, 4, 1), (PW, 1, 2, 1, 0),
-    (O, 0, -3, 2, 0), (PD, 0, 3, 1, 1), (PW, 1, -1, 4, 0), (PD, 0, 3, 1, 0), (PD, 0, -3, 1, 1), (PW, 1, 1, 4, 1),
-    (PW, 1, 1, 4, 0), (PD, 0, -3, 1, 0), (PD, 0, -1, 2, 1), (PICK, 1), (PICK, -1), (UNIT, 0, 0), (O, 0, 3, 2, 0),
-    (O, 0, 3, 2, 1), (PW, 1, 2, 2, 1), (PD, 0, 4, 1, 0), (PD, 0, 4, 1, 1), (CTX, 0, 2, 1), (CTX, 1, 2, 1),
-    (PD, 0, 2, 2, 0), (PW, 1, 2, 2, 0), (PICK, 2), (UNIT, 1, 0), (O, 0, 4, 2, 1), (O, 0, 4, 2, 0), (PD, 0, 3, 2, 1),
-    (PD, 0, -2, 2, 0), (PD, 0, -3, 2, 1), (PICK, 3), (PD, 0, 4, 2, 0), (PICK, -2), (PICK, -3), (PICK, 4),
-    (PW, 1, 2, 3, 1), (UNIT, 2, 0), (PW, 1, 2, 3, 0), (CTX, 0, 1, 2), (CTX, 1, 1, 2), (PW, 1, 2, 4, 1), (UNIT, 0, 1),
-    (PW, 1, 2, 4, 0), (UNIT, 3, 0), (PROJ, 0), (CTX, 0, 3, 1), (CTX, 1, 3, 1), (UNIT, 1, 1), (UNIT, 2, 1),
-    (UNIT, 3, 1), (PAIR, 0), (PROJ, 1), (CTX, 0, 2, 2), (CTX, 1, 2, 2), (PAIR, 1), (P1, 0, 0), (UNIT, 0, 2),
-    (CTX, 0, 3, 2), (CTX, 1, 3, 2), (UNIT, 1, 2), (UNIT, 2, 2), (P1, 0, 1), (UNIT, 3, 2), (PROJ, 2), (P2, 0),
-    (UNIT, 0, 3), (UNIT, 1, 3), (UNIT, 2, 3), (UNIT, 3, 3), (PAIR, 2), (P1, 1, 0), (PROJ, 3), (FIN, 0), (P1, 1, 1),
-    (PAIR, 3), (P2, 1), (P1, 2, 0), (P1, 2, 1), (FIN, 1), (P2, 2), (P1, 3, 0), (FIN, 2), (P1, 3, 1), (P2, 3),
-    (FIN, 3),
+    (PD, 1, 0, 1, 1), (PW, 0, 0, 1, 0), (PW, 0, 0, 1, 1), (O, 0, -1, 2, 0), (PW, 1, 0, 1, 0), (O, 0, -1, 2, 1),
+    (PD, 1, 0, 1, 0), (O, 1, 0, 3, 1), (CTX, 0, 0, 1), (CTX, 1, 0, 1), (O, 0, 1, 2, 0), (O, 0, 1, 2, 1),
+    (O, 1, 0, 4, 0), (PW, 0, 0, 2, 1), (PW, 0, 0, 2, 0), (PW, 1, 0, 2, 1), (PD, 1, 0, 2, 1), (PW, 1, -1, 1, 0),
+    (O, 0, -2, 1, 1), (O, 0, -2, 1, 0), (PD, 0, 0, 1, 1), (PW, 1, -1, 1, 1), (PD, 0, 0, 1, 0), (PW, 1, 1, 1, 0),
+    (CTX, 0, 2, 0), (CTX, 1, 2, 0), (PW, 1, 1, 1, 1), (PW, 1, 0, 2, 0), (O, 0, 2, 1, 1), (O, 0, 2, 1, 0),
+    (PD, 1, 0, 2, 0), (O, 1, 0, 4, 1), (PW, 1, 2, 1, 0), (O, 0, -3, 1, 1), (PW, 1, 2, 1, 1), (O, 0, -3, 1, 0),
+    (PD, 0, 1, 1, 1), (CTX, 0, 1, 1), (CTX, 1, 1, 1), (PD, 0, 1, 1, 0), (PD, 0, -1, 1, 1), (PD, 0, -1, 1, 0),
+    (PW, 1, -1, 2, 0), (PW, 1, 0, 3, 1), (PD, 1, 0, 3, 1), (PW, 1, 1, 2, 0), (O, 0, 3, 1, 1), (O, 0, 3, 1, 0),
+    (PD, 0, 2, 1, 1), (PW, 1, -1, 2, 1), (PD, 0, 2, 1, 0), (PW, 1, 0, 3, 0), (O, 0, -2, 2, 1), (CTX, 0, 3, 0),
+    (CTX, 1, 3, 0), (O, 0, -2, 2, 0), (PD, 1, 0, 3, 0), (PW, 1, 1, 2, 1), (PD, 0, 0, 2, 0), (O, 0, 2, 2, 1),
+    (PICK, 0), (PD, 0, -2, 1, 1), (O, 0, 2, 2, 0), (PW, 1, 2, 2, 0), (PW, 1, 2, 2, 1), (PD, 0, -2, 1, 0),
+    (PW, 1, 0, 4, 1), (PW, 1, -1, 3, 0), (O, 0, 4, 1, 1), (PW, 1, -1, 3, 1), (CTX, 0, 0, 2), (CTX, 1, 0, 2),
+    (O, 0, 4, 1, 0), (O, 0, -3, 2, 1), (PW, 1, 1, 3, 0), (PD, 0, 1, 2, 1), (PICK, 1), (O, 0, -3, 2, 0),
+    (PD, 0, -1, 2, 1), (PW, 1, 1, 3, 1), (PICK, -1), (PD, 0, 3, 1, 0), (PW, 1, 0, 4, 0), (PD, 0, 3, 1, 1),
+    (UNIT, 0, 0), (PD, 1, 0, 4, 0), (O, 0, 3, 2, 0), (O, 0, 3, 2, 1), (PW, 1, 2, 3, 1), (PD, 0, 2, 2, 0),
+    (PD, 0, -3, 1, 1), (PD, 0, -3, 1, 0), (PW, 1, 2, 3, 0), (PW, 1, -1, 4, 1), (CTX, 0, 2, 1), (CTX, 1, 2, 1),
+    (PD, 0, -2, 2, 0), (PW, 1, -1, 4, 0), (O, 0, 4, 2, 1), (PW, 1, 1, 4, 0), (PD, 0, 3, 2, 1), (PW, 1, 1, 4, 1),
+    (O, 0, 4, 2, 0), (PD, 0, 4, 1, 1), (PW, 1, 2, 4, 1), (PD, 0, 4, 1, 0), (PD, 0, -3, 2, 1), (PICK, 2), (PICK, -2),
+    (PICK, 3), (PICK, -3), (UNIT, 1, 0), (PW, 1, 2, 4, 0), (UNIT, 2, 0), (UNIT, 3, 0), (CTX, 0, 1, 2),
+    (CTX, 1, 1, 2), (PD, 0, 4, 2, 0), (PICK, 4), (PROJ, 0), (UNIT, 0, 1), (UNIT, 1, 1), (UNIT, 2, 1), (CTX, 0, 3, 1),
+    (CTX, 1, 3, 1), (PAIR, 0), (UNIT, 3, 1), (PROJ, 1), (CTX, 0, 2, 2), (CTX, 1, 2, 2), (P1, 0, 0), (PAIR, 1),
+    (UNIT, 0, 2), (UNIT, 1, 2), (P1, 0, 1), (UNIT, 2, 2), (CTX, 0, 3, 2), (CTX, 1, 3, 2), (UNIT, 3, 2), (P2, 0),
+    (PROJ, 2), (P1, 1, 0), (UNIT, 0, 3), (UNIT, 1, 3), (UNIT, 2, 3), (P1, 1, 1), (FIN, 0), (PAIR, 2), (UNIT, 3, 3),
+    (PROJ, 3), (P2, 1), (P1, 2, 0), (PAIR, 3), (P1, 2, 1), (FIN, 1), (P2, 2), (P1, 3, 0), (FIN, 2), (P1, 3, 1),
+    (P2, 3), (FIN, 3),
 )
 
 
@@ -97,8 +97,8 @@
 
 
 def fused_kernel(
-    ctx_ref, weight_ref, side_ref, gain_ref, res_hbm, f_hbm, g_hbm, targets_hbm, o_ref, f_out, g_out,
-    pack_ref, res_ref, f_ref, g_ref, targets_ref, wbuf, cbuf, down, acc, part, pair, line, up_in, down_in, sums,
+    ctx_hbm, weight_hbm, side_hbm, gain_hbm, res_hbm, f_hbm, g_hbm, targets_hbm, o_ref, f_out, g_out,
+    ctx_ref, weight_ref, side_ref, gain_ref, pack_ref, res_ref, f_ref, g_ref, targets_ref, wbuf, cbuf, down, acc, part, pair, line, up_in, down_in, sums, columns, tiles, tiles_in, tiles_sum, tiles_far,
     grads, buf0, summed, buf_a, mid, buf_b, buf_x, tail, fin, local, send_sems, recv_sems
 ):
     y, x, z, c = position()
@@ -109,6 +109,7 @@
     y_dev = (device((y + 1) % 8, x, z, c), device((y + 7) % 8, x, z, c))
     x_dev = (device(y, (x + 1) % 4, z, c), device(y, (x + 3) % 4, z, c))
     z_dev = (device(y, x, (z + 1) % 8, c), device(y, x, (z + 7) % 8, c))
+    chip_dev = [device(y, x, z - j + (j + d) % 4, c) for d in (1, 2, 3)]
     z_far = device(y, x, (z + 4) % 8, c)
 
     on_z = 1 - c
@@ -132,11 +133,22 @@
     loads = [
         pltpu.make_async_copy(src, dst, local.at[2 + i])
         for i, (src, dst) in enumerate(
-            ((res_hbm, res_ref), (f_hbm, f_ref), (g_hbm, g_ref), (targets_hbm, targets_ref))
+            (
+                (weight_hbm, weight_ref),
+                (side_hbm, side_ref),
+                (ctx_hbm, ctx_ref),
+                (gain_hbm, gain_ref),
+                (res_hbm, res_ref),
+                (f_hbm, f_ref),
+                (g_hbm, g_ref),
+                (targets_hbm, targets_ref),
+            )
         )
     ]
     for load in loads:
         load.start()
+    for load in loads[:4]:
+        load.wait()
     pack_ref[0:48, :] = weight_ref[...]
     pack_ref[48:64, :] = jnp.zeros((16, 768), jnp.bfloat16)
     pack_ref[48:60, :] = side_ref[...]
@@ -145,6 +157,7 @@
     slots = {}
     sent = []
     begun = set()
+    held = []
 
     def remote(key, src, dst, to):
         at = slots.setdefault(key, len(slots))
@@ -156,8 +169,15 @@
         if chips is None:
             action()
             return
-        for chip in chips:
-            pl.when(j == chip)(action)
+        low, high = min(chips), max(chips)
+        if low == high:
+            pl.when(j == low)(action)
+        elif high == 3:
+            pl.when(j >= low)(action)
+        elif low == 0:
+            pl.when(j <= high)(action)
+        else:
+            pl.when((j >= low) & (j <= high))(action)
 
     def send(key, make, chips=None):
         only(chips, lambda: remote(key, *make()).start())
@@ -182,6 +202,9 @@
             send(key, lambda: (block(kind, dy, dx, span), block(kind, dy, dx, span), to))
 
     def start_x(kind, dy):
+        if PW not in begun and (kind == PD or abs(dy) >= 2):
+            held.append((kind, dy))
+            return
         for s in (0, 1):
             send_block((kind, 0, dy, 1, s), kind, dy, 0, x_dev[s])
 
@@ -240,6 +263,10 @@
         if s == 1:
             send_block((PW, 0, 0, 2, side), PW, 0, dx, x_dev[side], span)
             start_y(dx)
+            if after_both(key):
+                begun.add(PW)
+                for item in held:
+                    start_x(*item)
         elif after_both(key):
             start_y(2)
 
@@ -262,10 +289,17 @@
         chips = reach(side, h)
         region = lambda: lanes(t, source(side, h) * 2 + c)
         onward = [k for k in chips if (k < 3 if side == 0 else k > 0)]
-        only(chips, lambda: wait(key, region()))
-        if onward:
-            send((CTX, side, t, h + 1), lambda: (region(), region(), z_dev[side]), onward)
-        send((CTX, side + 2, t, h), lambda: (region(), region(), sibling), chips)
+        further = (CTX, side, t, h + 1), lambda: (region(), region(), z_dev[side]), onward
+        share = (CTX, side + 2, t, h), lambda: (region(), region(), sibling), chips
+
+        def arrived():
+            wait(key, region())
+            if onward:
+                only(onward, lambda: remote(further[0], *further[1]()).start())
+            remote(share[0], *share[1]()).start()
+
+        only(chips, arrived)
+        sent.extend([further, share] if onward else [share])
         if h == 0 and t + LEAD < CHUNKS:
             own_ctx(t + LEAD, side, (1, 2))
 
@@ -314,8 +348,8 @@
         here = pl.ds(t * ROWS, ROWS)
         if PROJ not in begun:
             begun.add(PROJ)
-            loads[0].wait()
-        gain = gain_ref[...].astype(jnp.float32)
+            loads[4].wait()
+        gain = gain_ref[...].astype(jnp.float32).reshape(1, 768)
         stream = (res_ref[:, here, :].reshape(8 * ROWS, 768).astype(jnp.float32) + acc[t]).astype(jnp.bfloat16)
         value = stream.astype(jnp.float32)
         total = jnp.sum(value, axis=1, keepdims=True)
@@ -326,31 +360,52 @@
         stats = jnp.where(column == 0, total, jnp.where(column == 1, squares, 0.0))
         for k in range(8):
             cut = slice(k * ROWS, (k + 1) * ROWS)
-            part[t, k % 2, k // 2, 0:ROWS, 0:768] = mapped[cut]
-            part[t, k % 2, k // 2, 0:ROWS, 768:896] = stats[cut]
-        if t == 0:
-            rows = jnp.broadcast_to(gain, (16, 768)).astype(jnp.bfloat16)
-            gain_rows = lax.dot_general(rows, down[...], (((1,), (1,)), ((), ())), preferred_element_type=jnp.float32)
-            for k in range(8):
-                part[0, k % 2, k // 2, ROWS:ROWS + 8, 0:768] = gain_rows[0:8]
-                part[0, k % 2, k // 2, ROWS:ROWS + 8, 768:896] = jnp.zeros((8, 128), jnp.float32)
-        rows_sent = pl.ds(0, tall(t))
-        send((PAIR, t), lambda: (part.at[t, 1 - c, :, rows_sent], pair.at[t, :, rows_sent], sibling))
-
-    def tall(t):
-        return ROWS + 8 if t == 0 else ROWS
+            part[t, k % 2, k // 2] = mapped[cut]
+            columns[k, here, :] = stats[cut]
+        begun.add((PROJ, t))
+        send((PAIR, t), lambda: (part.at[t, 1 - c], pair.at[t], sibling))
+        if all((PROJ, k) in begun for k in range(CHUNKS)):
+            stats_start(gain)
+
+    def stats_start(gain):
+        rows = jnp.broadcast_to(gain, (16, 768)).astype(jnp.bfloat16)
+        shares = lax.dot_general(rows, down[...], (((1,), (1,)), ((), ())), preferred_element_type=jnp.float32)
+        row = lax.broadcasted_iota(jnp.int32, (8, 128), 0)
+        lower = jnp.zeros((8, 128), jnp.float32)
+        for i in range(6):
+            lower = jnp.where(row == i + 2, shares[0:8, i * 128:(i + 1) * 128], lower)
+        for k in range(8):
+            tiles[k % 2, k // 2] = jnp.where(row < 2, jnp.transpose(columns[k])[0:8, :], lower)
+        send((STAT, 0), lambda: (tiles.at[1 - c], tiles_in, sibling))
+
+    def stats_pass():
+        wait((STAT, 0), tiles_in)
+        tiles_sum[...] = tiles[c] + tiles_in[...]
+        for d in (2, 1, 3):
+            send((STAT, d), lambda d=d: (tiles_sum.at[(j + d) % 4], tiles_far.at[d - 1], chip_dev[d - 1]))
+
+    def stats_end():
+        total = tiles_sum[j]
+        for d in (2, 1, 3):
+            wait((STAT, d), tiles_far.at[d - 1])
+            total = total + tiles_far[d - 1]
+        return jnp.transpose(jnp.concatenate([total, jnp.zeros((120, 128), jnp.float32)], axis=0)), jnp.concatenate(
+            [total[i + 2:i + 3, :] for i in range(6)], axis=1
+        )
 
     def piece(ref, t, dest):
-        return ref.at[t, dest, pl.ds(0, tall(t))]
+        return ref.at[t, dest]
 
     def add_pair(key):
         t = key[1]
-        rows = pl.ds(0, tall(t))
-        wait(key, pair.at[t, :, rows])
-        line[t, :, rows] = part[t, c, :, rows] + pair[t, :, rows]
+        wait(key, pair.at[t])
+        line[t] = part[t, c] + pair[t]
         for i in range(3):
             pass_on(t, 0, 0, 3 - i, True)
             pass_on(t, 3, 1, i, True)
+        begun.add(key)
+        if all((PAIR, k) in begun for k in range(CHUNKS)):
+            stats_pass()
 
     def pass_on(t, chip, side, dest, first=False):
         kind, arrived = ((UP, up_in), (DOWN, down_in))[side]
@@ -358,7 +413,7 @@
 
             def add():
                 wait((kind, t, dest), piece(arrived, t, dest))
-                line[t, dest, 0:tall(t)] += arrived[t, dest, 0:tall(t)]
+                line[t, dest] += arrived[t, dest]
 
             only((chip,), add)
         send((kind, t, dest), lambda: (piece(line, t, dest), piece(arrived, t, dest), z_dev[side]), (chip,))
@@ -368,16 +423,14 @@
         for chip in range(4):
 
             def add():
-                total = line[t, chip, 0:tall(t)]
+                total = line[t, chip]
                 if chip > 0:
                     wait((UP, t, chip), piece(up_in, t, chip))
-                    total = total + up_in[t, chip, 0:tall(t)]
+                    total = total + up_in[t, chip]
                 if chip < 3:
                     wait((DOWN, t, chip), piece(down_in, t, chip))
-                    total = total + down_in[t, chip, 0:tall(t)]
-                sums[t * ROWS:(t + 1) * ROWS, :] = total[0:ROWS]
-                if t == 0:
-                    sums[128:136, :] = total[ROWS:ROWS + 8]
+                    total = total + down_in[t, chip]
+                sums[t * ROWS:(t + 1) * ROWS, :] = total
 
             only((chip,), add)
 
@@ -401,14 +454,20 @@
         else:
             {PICK: pick, UNIT: unit, PROJ: project, PAIR: add_pair, FIN: finish}[kind](key)
 
+    def drain():
+        for key, make, chips in sent:
+            only(chips, lambda: remote(key, *make()).wait_send())
+        sent.clear()
+
     def side_block():
-        for load in loads[1:]:
+        for load in loads[5:]:
             load.wait()
-        mean = sums[0:128, 768:769] * (1.0 / (8 * 768))
-        spread = sums[0:128, 769:770] * (1.0 / (8 * 768)) - mean * mean
+        stats, gain_map = stats_end()
+        mean = stats[:, 0:1] * (1.0 / (8 * 768))
+        spread = stats[:, 1:2] * (1.0 / (8 * 768)) - mean * mean
         scale = 1.0 / jnp.sqrt(spread + 1e-06)
-        first = (sums[0:128, 0:384] - mean * sums[128:129, 0:384]) * scale
-        second = (sums[0:128, 384:768] - mean * sums[128:129, 384:768]) * scale
+        first = (sums[0:128, 0:384] - mean * gain_map[:, 0:384]) * scale
+        second = (sums[0:128, 384:768] - mean * gain_map[:, 384:768]) * scale
         bend, f_slope = gelu_and_slope(exact_dot(second, f_ref[...], 0))
         upper = first + bend
         bend, g_slope = gelu_and_slope(exact_dot(upper, g_ref[...], 0))
@@ -431,6 +490,10 @@
         summed[...] = grads[c] + buf0[...]
         for d in FAR_FIRST:
             send((GRAD, d), lambda d=d: (rows_of(summed, (pos_a + d) % 8, 48), buf_a.at[d - 1], along_a(d)))
+        earlier, later = sent[:-8], sent[-8:]
+        sent[:] = earlier
+        drain()
+        sent.extend(later)
         total = summed[pl.ds(pl.multiple_of(pos_a * 48, 8), 48), :]
         for d in FAR_FIRST:
             wait((GRAD, d), buf_a.at[d - 1])
@@ -486,24 +549,26 @@
         task(key)
     side_block()
     gradient_sum()
-    for key, make, chips in sent:
-        only(chips, lambda: remote(key, *make()).wait_send())
+    drain()
 
 
 def fused(context, out_weight, side_down, ln_gain, residual, f_weight, g_weight, targets):
     vmem = pl.BlockSpec(memory_space=pltpu.VMEM)
-    away = pl.BlockSpec(memory_space=pl.ANY)
-    tall = ROWS + 8
+    away = pl.BlockSpec(memory_space=pltpu.HBM)
     f32 = jnp.float32
     bf16 = jnp.bfloat16
-    piece = pltpu.VMEM((CHUNKS, 4, tall, WIDTH), f32)
+    piece = pltpu.VMEM((CHUNKS, 4, ROWS, WIDTH), f32)
     square = jax.ShapeDtypeStruct((384, 384), f32)
     return pl.pallas_call(
         fused_kernel,
         out_shape=(jax.ShapeDtypeStruct((128, 768), f32), square, square),
-        in_specs=[vmem] * 4 + [away] * 4,
+        in_specs=[away] * 8,
         out_specs=(vmem, vmem, vmem),
         scratch_shapes=[
+            pltpu.VMEM((8, 128, 384), bf16),
+            pltpu.VMEM((48, 768), bf16),
+            pltpu.VMEM((12, 768), bf16),
+            pltpu.VMEM((768,), bf16),
             pltpu.VMEM((64, 768), bf16),
             pltpu.VMEM((8, 128, 768), bf16),
             pltpu.VMEM((384, 384), bf16),
@@ -513,12 +578,17 @@
             pltpu.VMEM((8, 128, 3072), bf16),
             pltpu.VMEM((768, 768), bf16),
             pltpu.VMEM((CHUNKS, 8 * ROWS, 768), f32),
-            pltpu.VMEM((CHUNKS, 2, 4, tall, WIDTH), f32),
+            pltpu.VMEM((CHUNKS, 2, 4, ROWS, WIDTH), f32),
             piece,
             piece,
             piece,
             piece,
-            pltpu.VMEM((136, WIDTH), f32),
+            pltpu.VMEM((128, WIDTH), f32),
+            pltpu.VMEM((8, 128, 128), f32),
+            pltpu.VMEM((2, 4, 8, 128), f32),
+            pltpu.VMEM((4, 8, 128), f32),
+            pltpu.VMEM((4, 8, 128), f32),
+            pltpu.VMEM((3, 8, 128), f32),
             pltpu.VMEM((2, 384, 384), f32),
             pltpu.VMEM((384, 384), f32),
             pltpu.VMEM((384, 384), f32),
@@ -528,20 +598,45 @@
             pltpu.VMEM((4, 8, 384), f32),
             pltpu.VMEM((64, 384), f32),
             pltpu.VMEM((2, 384, 384), f32),
-            pltpu.SemaphoreType.DMA((6,)),
+            pltpu.SemaphoreType.DMA((10,)),
             pltpu.SemaphoreType.DMA((SLOTS,)),
             pltpu.SemaphoreType.DMA((SLOTS,)),
         ],
         compiler_params=pltpu.CompilerParams(collective_id=0, has_side_effects=True, vmem_limit_bytes=60 * 1024 * 1024),
         name="fused_layer",
     )(
-        context.reshape(8, 128, 384), out_weight, side_down.T, ln_gain.reshape(1, 768), residual.reshape(8, 128, 768),
+        context.reshape(8, 128, 384), out_weight, side_down.T, ln_gain, residual.reshape(8, 128, 768),
         f_weight, g_weight, targets,
     )
 
 
+def hand_over(a_ref, b_ref, c_ref, a_out, b_out, c_out, a_kept, b_kept, c_kept, sems):
+    steps = [
+        (pltpu.make_async_copy(src, kept, sems.at[0, i]), pltpu.make_async_copy(kept, dst, sems.at[1, i]))
+        for i, (src, kept, dst) in enumerate(
+            ((a_ref, a_kept, a_out), (b_ref, b_kept, b_out), (c_ref, c_kept, c_out))
+        )
+    ]
+    for load, _ in steps:
+        load.start()
+    for load, store in steps:
+        load.wait()
+        store.start()
+    for _, store in steps:
+        store.wait()
+
+
 def per_device(context, out_weight, residual, ln_gain, side_down, f_weight, g_weight, targets):
-    return fused(context, out_weight, side_down, ln_gain, residual, f_weight, g_weight, targets)
+    results = fused(context, out_weight, side_down, ln_gain, residual, f_weight, g_weight, targets)
+    away = pl.BlockSpec(memory_space=pltpu.HBM)
+    return pl.pallas_call(
+        hand_over,
+        out_shape=tuple(jax.ShapeDtypeStruct(r.shape, r.dtype) for r in results),
+        in_specs=[away] * 3,
+        out_specs=(away,) * 3,
+        scratch_shapes=[pltpu.VMEM(r.shape, r.dtype) for r in results] + [pltpu.SemaphoreType.DMA((2, 3))],
+        name="hand_over",
+    )(*results)
 
 
 def solution(mesh):

time: 153 us -> 140 us (0.915)
  Pallas kernels: 146 us -> 139 us
  local copies, waits for them, and re-layouts: 5.83 us -> 0 us
    pallas_call x1, Pallas kernels: 146 us -> 136 us  [fused(): pl.pallas_call(fused_kernel, out_shape=(jax.ShapeDtypeStruct((128, 768),...]
    unnamed x5 -> x0, local copies, waits for them, and re-layouts: 4.56 us -> none
    pallas_call x0 -> x1, Pallas kernels: none -> 2.25 us  [per_device(): pl.pallas_call(hand_over, out_shape=tuple((jax.ShapeDtypeStruct(r.shape,...]
where the time goes in v3:
time: 140 us
  Pallas kernels  139 us (99%)
    pallas_call x1, Pallas kernels, fused(): pl.pallas_call(fused_kernel, out_shape=(jax.ShapeDtypeStruct((128, 768),...  136 us

profile of v3, /device:TPU:1, one launch (start us, length us, event | category | flops | bytes accessed | tf_op | source)
XLA Modules:
  0.0 139.5 jit_solution(1800108866829602006)
XLA Ops:
  0.6 136.5 %fused_layer.1 = (f32[128,768]{1,0:T(8,128)}, f32[384,384]{1,0:T(8,128)}, f32[384,384]{1,0:T(8,128)}) custom-call(bf16[8,128,384]{2,1,0:T(8,128)(2,1)} %bitcast.4, bf16[48,768]{1,0:T(8,128)(2,1)} %weight_hbm.1, bf16[12,768]{1,0:T(8,128)(2,1)} %bitcast.5, bf16[768]{0:T(1024)(128)(2,1)} %gain_hbm.1, bf16[8,128,768]{2,1,0:T(8,128)(2,1)} %bitcast.3, ...), custom_call_target="tpu_custom_call" | custom-call | tf_op jit(solution)/shard_map/fused_layer/pallas_call | solution.py:562
  137.1 2.2 %hand_over.1 = (f32[128,768]{1,0:T(8,128)}, f32[384,384]{1,0:T(8,128)}, f32[384,384]{1,0:T(8,128)}) custom-call(f32[128,768]{1,0:T(8,128)} %get-tuple-element.6.a_ref, f32[384,384]{1,0:T(8,128)} %get-tuple-element.7.b_ref, f32[384,384]{1,0:T(8,128)} %get-tuple-element.8.c_ref), custom_call_target="tpu_custom_call" | custom-call | tf_op jit(solution)/shard_map/hand_over/pallas_call | solution.py:632

commit v4 on v3

--- a/solution.py
+++ b/solution.py
@@ -169,6 +169,9 @@
         if chips is None:
             action()
             return
+        if callable(chips):
+            pl.when(chips())(action)
+            return
         low, high = min(chips), max(chips)
         if low == high:
             pl.when(j == low)(action)
@@ -484,53 +487,77 @@
     def rows_of(ref, at, count):
         return ref.at[pl.ds(pl.multiple_of(at * count, 8), count)]
 
+    def owned(at, h):
+        return pl.ds(pl.multiple_of(at * 48 + 24 * h, 8), 24)
+
+    def third(at, h):
+        return (at >= 3 * h) & (at < 3 * h + 3)
+
+    def reducer():
+        return pos_b < 6
+
+    def there(h, d, core, far):
+        base = far * y + (1 - far) * z
+        return fin.at[core, owned((base + 8 - d) % 8, h)]
+
     def gradient_sum():
         send((GRAD, 0), lambda: (grads.at[1 - c], buf0, sibling))
         wait((GRAD, 0), buf0)
         summed[...] = grads[c] + buf0[...]
-        for d in FAR_FIRST:
-            send((GRAD, d), lambda d=d: (rows_of(summed, (pos_a + d) % 8, 48), buf_a.at[d - 1], along_a(d)))
-        earlier, later = sent[:-8], sent[-8:]
+        for h in (0, 1):
+            for d in FAR_FIRST:
+                send((GRAD, 1, h, d), lambda h=h, d=d: (summed.at[owned((pos_a + d) % 8, h)], buf_a.at[h, d - 1], along_a(d)))
+        earlier, later = sent[:-15], sent[-15:]
         sent[:] = earlier
         drain()
         sent.extend(later)
-        total = summed[pl.ds(pl.multiple_of(pos_a * 48, 8), 48), :]
+        for h in (0, 1):
+            total = summed[owned(pos_a, h), :]
+            for d in FAR_FIRST:
+                wait((GRAD, 1, h, d), buf_a.at[h, d - 1])
+                total = total + buf_a[h, d - 1]
+            mid[24 * h:24 * h + 24, :] = total
+            for d in FAR_FIRST:
+                send(
+                    (GRAD, 2, d),
+                    lambda d=d: (rows_of(mid, (pos_b + d) % 8, 8), buf_b.at[d - 1], along_b(d)),
+                    lambda d=d, h=h: third((pos_b + d) % 8, h),
+                )
+
+        def reduce():
+            total = mid[pl.ds(pl.multiple_of(pos_b * 8, 8), 8), :]
+            for d in FAR_FIRST:
+                wait((GRAD, 2, d), buf_b.at[d - 1])
+                total = total + buf_b[d - 1]
+            buf_x[x] = total
+
+        only(reducer, reduce)
+        for d in (2, 1, 3):
+            send((GRAD, 3, d), lambda d=d: (buf_x.at[x], buf_x.at[x], along_x(d)), reducer)
+
+        def cross():
+            for d in (2, 1, 3):
+                wait((GRAD, 3, d), buf_x.at[(x + 4 - d) % 4])
+            tail[pl.ds(pl.multiple_of(pos_b * 8, 8), 8), :] = (buf_x[0] + buf_x[1]) + (buf_x[2] + buf_x[3])
+
+        only(reducer, cross)
         for d in FAR_FIRST:
-            wait((GRAD, d), buf_a.at[d - 1])
-            total = total + buf_a[d - 1]
-        mid[0:48, :] = total
-        mid[48:64, :] = jnp.zeros((16, 384), jnp.float32)
-        for d in FAR_FIRST:
-            send((GRAD, 7 + d), lambda d=d: (rows_of(mid, (pos_b + d) % 8, 8), buf_b.at[d - 1], along_b(d)))
-        total = mid[pl.ds(pl.multiple_of(pos_b * 8, 8), 8), :]
-        for d in FAR_FIRST:
-            wait((GRAD, 7 + d), buf_b.at[d - 1])
-            total = total + buf_b[d - 1]
-        buf_x[x] = total
-        for d in (2, 1, 3):
-            send((GRAD, 14 + d), lambda d=d: (buf_x.at[x], buf_x.at[x], along_x(d)))
-        for d in (2, 1, 3):
-            wait((GRAD, 14 + d), buf_x.at[(x + 4 - d) % 4])
-        tail[pl.ds(pl.multiple_of(pos_b * 8, 8), 8), :] = (buf_x[0] + buf_x[1]) + (buf_x[2] + buf_x[3])
-        for d in FAR_FIRST:
-            send((GRAD, 17 + d), lambda d=d: (rows_of(tail, pos_b, 8), rows_of(tail, pos_b, 8), along_b(d)))
-        for d in FAR_FIRST:
-            wait((GRAD, 17 + d), rows_of(tail, (pos_b + 8 - d) % 8, 8))
-        for d in FAR_FIRST:
-            send((GRAD, 24 + d), lambda d=d: (tail.at[pl.ds(0, 48)], fin.at[c, pl.ds(pl.multiple_of(pos_a * 48, 8), 48)], along_a(d)))
-        send((GRAD, 32), lambda: (tail.at[pl.ds(0, 48)], fin.at[c, pl.ds(pl.multiple_of(pos_a * 48, 8), 48)], sibling))
-        fin[c, pl.ds(pl.multiple_of(pos_a * 48, 8), 48), :] = tail[0:48, :]
-
-        def there(d, core, far):
-            base = far * y + (1 - far) * z
-            return fin.at[core, pl.ds(pl.multiple_of((base + 8 - d) % 8 * 48, 8), 48)]
-
-        for d in NEAR_FIRST:
-            wait((GRAD, 24 + d), there(d, c, c))
-            send((GRAD, 32 + d), lambda d=d: (there(d, c, c), there(d, c, c), sibling))
-        wait((GRAD, 32), there(0, 1 - c, 1 - c))
-        for d in NEAR_FIRST:
-            wait((GRAD, 32 + d), there(d, 1 - c, 1 - c))
+            send((GRAD, 4, d), lambda d=d: (rows_of(tail, pos_b, 8), rows_of(tail, pos_b, 8), along_b(d)), reducer)
+        for h in (0, 1):
+            for d in NEAR_FIRST:
+                owner = (pos_b + 8 - d) % 8
+                only(lambda: third(owner, h), lambda: wait((GRAD, 4, d), rows_of(tail, owner, 8)))
+            for d in FAR_FIRST:
+                send((GRAD, 5, h, d), lambda h=h, d=d: (tail.at[pl.ds(24 * h, 24)], fin.at[c, owned(pos_a, h)], along_a(d)))
+            send((GRAD, 6, h, 0), lambda h=h: (tail.at[pl.ds(24 * h, 24)], fin.at[c, owned(pos_a, h)], sibling))
+            fin[c, owned(pos_a, h), :] = tail[24 * h:24 * h + 24, :]
+        for h in (0, 1):
+            for d in NEAR_FIRST:
+                wait((GRAD, 5, h, d), there(h, d, c, c))
+                send((GRAD, 6, h, d), lambda h=h, d=d: (there(h, d, c, c), there(h, d, c, c), sibling))
+        for h in (0, 1):
+            for d in (0,) + NEAR_FIRST:
+                wait((GRAD, 6, h, d), there(h, d, 1 - c, 1 - c))
         f_out[...] = fin[0]
         g_out[...] = fin[1]
 
@@ -592,11 +619,11 @@
             pltpu.VMEM((2, 384, 384), f32),
             pltpu.VMEM((384, 384), f32),
             pltpu.VMEM((384, 384), f32),
-            pltpu.VMEM((7, 48, 384), f32),
-            pltpu.VMEM((64, 384), f32),
+            pltpu.VMEM((2, 7, 24, 384), f32),
+            pltpu.VMEM((48, 384), f32),
             pltpu.VMEM((7, 8, 384), f32),
             pltpu.VMEM((4, 8, 384), f32),
-            pltpu.VMEM((64, 384), f32),
+            pltpu.VMEM((48, 384), f32),
             pltpu.VMEM((2, 384, 384), f32),
             pltpu.SemaphoreType.DMA((10,)),
             pltpu.SemaphoreType.DMA((SLOTS,)),

time: 140 us -> 137 us (0.979)
  Pallas kernels: 139 us -> 136 us
    pallas_call x1, Pallas kernels: 136 us -> 134 us  [fused(): pl.pallas_call(fused_kernel, out_shape=(jax.ShapeDtypeStruct((128, 768),...]
where the time goes in v4:
time: 137 us
  Pallas kernels  136 us (99%)
    pallas_call x1, Pallas kernels, fused(): pl.pallas_call(fused_kernel, out_shape=(jax.ShapeDtypeStruct((128, 768),...  134 us

profile of v4, /device:TPU:1, one launch (start us, length us, event | category | flops | bytes accessed | tf_op | source)
XLA Modules:
  0.0 136.9 jit_solution(17518583819154206955)
XLA Ops:
  0.6 133.9 %fused_layer.1 = (f32[128,768]{1,0:T(8,128)}, f32[384,384]{1,0:T(8,128)}, f32[384,384]{1,0:T(8,128)}) custom-call(bf16[8,128,384]{2,1,0:T(8,128)(2,1)} %bitcast.4, bf16[48,768]{1,0:T(8,128)(2,1)} %weight_hbm.1, bf16[12,768]{1,0:T(8,128)(2,1)} %bitcast.5, bf16[768]{0:T(1024)(128)(2,1)} %gain_hbm.1, bf16[8,128,768]{2,1,0:T(8,128)(2,1)} %bitcast.3, ...), custom_call_target="tpu_custom_call" | custom-call | tf_op jit(solution)/shard_map/fused_layer/pallas_call | solution.py:589
  134.5 2.2 %hand_over.1 = (f32[128,768]{1,0:T(8,128)}, f32[384,384]{1,0:T(8,128)}, f32[384,384]{1,0:T(8,128)}) custom-call(f32[128,768]{1,0:T(8,128)} %get-tuple-element.6.a_ref, f32[384,384]{1,0:T(8,128)} %get-tuple-element.7.b_ref, f32[384,384]{1,0:T(8,128)} %get-tuple-element.8.c_ref), custom_call_target="tpu_custom_call" | custom-call | tf_op jit(solution)/shard_map/hand_over/pallas_call | solution.py:659
